TPU v7x, 32 devices: a whole 2x2x4 slice. The times are simulated.
32 devices in a mesh: alpha: 4 (over y, core), beta: 8 (over z, x).
Axes of the slice: x: 2, y: 2, z: 4, core: 2. Of those that a mesh axis runs over, the one named last changes fastest.
Arguments:
- coeff: float32 [128, 1024], P('alpha', 'beta'), may hold values from -6 to 6
- integrals: float32 [528, 528], replicated, as said below
- beta_pairs: int32 [1024, 230], P('beta'), may hold values from 0 to 527, as said below
- beta_targets: int32 [1024, 230], P('beta'), may hold values from 0 to 1023
- beta_signs: int32 [1024, 230], P('beta'), may hold values from -1 to 1, as said below
- alpha_pairs: int32 [128, 230], P('alpha'), may hold values from 0 to 527, as said below
- alpha_targets: int32 [128, 230], P('alpha'), may hold values from 0 to 127
- alpha_signs: int32 [128, 230], P('alpha'), may hold values from -1 to 1, as said below
Outputs:
- sigma: float32 [128, 1024], P('alpha', 'beta')
Inputs may be any that keep to these rules, and one draw needn't show every extreme that they name: The 230 pairs of one row of beta_pairs are distinct. `beta_signs`: each sign is -1 or 1. The 230 pairs of one row of alpha_pairs are distinct. `alpha_signs`: each sign is -1 or 1. `integrals`: symmetric.
All inputs are finite; a program needn't handle non-finite values.
Results may differ from a plain program's by a relative error of at most 0.0003.
Values sent between devices are 32-bit elements; how exact they have to be, the bound alone decides.
No kernel may reach another device: no remote copies, remote signals or barrier semaphores. Data moves between devices by JAX's collectives and lax.ppermute only.
A program may use at most 128 MiB of HBM per device.

v0:
```python
import jax
import jax.numpy as jnp
from jax import lax
from jax.sharding import PartitionSpec as P

PAIRS = 528


def local(
    coeff, integrals, beta_pairs, beta_targets, beta_signs, alpha_pairs, alpha_targets, alpha_signs
):
    rows_here = coeff.shape[0]
    cols_here = coeff.shape[1]
    total_rows = rows_here * lax.axis_size("alpha")
    width = (PAIRS + 127) // 128 * 128
    padded_ints = jnp.zeros((width, width), jnp.float32).at[:PAIRS, :PAIRS].set(integrals)
    gathered = lax.all_gather(coeff, "beta", axis=1, tiled=True)
    by_column = jnp.transpose(gathered)
    block = min(16, cols_here)
    count = cols_here // block
    pair_ids = jnp.arange(width, dtype=jnp.int32)
    string_ids = jnp.arange(total_rows, dtype=jnp.int32)
    alpha_onehot = (alpha_pairs[:, :, None] == pair_ids[None, None, :]).astype(jnp.float32)
    alpha_onehot = alpha_onehot * alpha_signs.astype(jnp.float32)[:, :, None]
    target_onehot = (alpha_targets[:, :, None] == string_ids[None, None, :]).astype(jnp.float32)
    fold = jnp.einsum(
        "aeq,aei->aqi",
        alpha_onehot,
        target_onehot,
        precision=lax.Precision.HIGHEST,
        preferred_element_type=jnp.float32,
    ).reshape(rows_here * width, total_rows)

    def block_terms(start):
        targets = lax.dynamic_slice_in_dim(beta_targets, start, block, 0)
        pairs = lax.dynamic_slice_in_dim(beta_pairs, start, block, 0)
        signs = lax.dynamic_slice_in_dim(beta_signs, start, block, 0).astype(jnp.float32)
        values = jnp.take(by_column, targets.reshape(-1), axis=0).reshape(
            block, targets.shape[1], rows_here
        )
        beta_onehot = (pairs[:, :, None] == pair_ids[None, None, :]).astype(jnp.float32) * signs[
            :, :, None
        ]
        lifted = jnp.einsum(
            "bea,bep->bap",
            values,
            beta_onehot,
            precision=lax.Precision.HIGHEST,
            preferred_element_type=jnp.float32,
        )
        mixed = jnp.dot(
            lifted.reshape(-1, width),
            padded_ints,
            precision=lax.Precision.HIGHEST,
            preferred_element_type=jnp.float32,
        ).reshape(block, rows_here * width)
        return jnp.einsum(
            "bm,mi->ib",
            mixed,
            fold,
            precision=lax.Precision.HIGHEST,
            preferred_element_type=jnp.float32,
        )

    def step_after(index, partial_value):
        start = (index * block).astype(jnp.int32)
        return lax.dynamic_update_slice_in_dim(partial_value, block_terms(start), start, 1)

    partial_value = lax.fori_loop(
        0, count, step_after, jnp.zeros((total_rows, cols_here), jnp.float32)
    )
    return lax.psum_scatter(partial_value, "alpha", scatter_dimension=0, tiled=True)


def solution(mesh):
    placed = (
        P("alpha", "beta"),
        P(),
        P("beta", None),
        P("beta", None),
        P("beta", None),
        P("alpha", None),
        P("alpha", None),
        P("alpha", None),
    )
    return jax.shard_map(
        local, mesh=mesh, in_specs=placed, out_specs=P("alpha", "beta"), check_vma=False
    )
```

profile of v0, /device:TPU:0, one launch (start us, length us, event | category | flops | bytes accessed | tf_op | source)
XLA Modules:
  0.0 327.1 jit_solution(11085611916219268635)
XLA Ops:
  11.2 33.0 %all_gather.3 = f32[32,1024]{0,1:T(8,128)S(1)} all-gather(f32[32,128]{0,1:T(8,128)S(1)} %copy.17), channel_id=1, replica_groups=mesh['alpha'=4,'beta'=8] {'beta'}, dimensions={1}, use_global_device_ids=true | all-gather | bytes 147456 | tf_op jit(solution)/shard_map/all_gather | solution.py:17
  45.6 24.5 %fusion.11 = f32[32,640,128]{2,1,0:T(8,128)} fusion(f32[32,230]{1,0:T(8,128)S(1)} %convert_element_type.15, s32[32,230]{1,0:T(8,128)S(1)} %copy-done.2, s32[32,230]{1,0:T(8,128)S(1)} %copy-done.3), kind=kOutput, calls=%fused_computation.21 | convolution fusion | flops 7245537280 | bytes 10574080 | tf_op jit(solution)/shard_map/aeq,aei->aqi/dot_general | solution.py:26
  70.7 227.1 %while.15 = (s32[]{:T(128)}, f32[128,128]{0,1:T(8,128)}, s32[128,230]{1,0:T(8,128)S(1)}, f32[1024,32]{1,0:T(8,128)S(1)}, s32[128,230]{1,0:T(8,128)S(1)}, /*index...) while((s32[]{:T(128)}, f32[128,128]{0,1:T(8,128)}, ...), condition=%wide.region_1.2_spmd.clone, body=%wide.region_0.0_spmd.clone.sunk | while | flops 3929164800 | bytes 31019660 | solution.py:69
  70.9 6.3 %gather_fusion = f32[3680,32]{1,0:T(8,128)S(1)} fusion(f32[1024,32]{1,0:T(8,128)S(1)} %get-tuple-element.310, s32[4096]{0:T(1024)S(1)} %pad_clamp_fusion.2), kind=kCustom, calls=%fused_computation.clone.clone.1 | custom fusion | bytes 956800 | tf_op jit(solution)/shard_map/while/body/eval_jaxpr/jit(_take)/gather | solution.py:38
  78.7 8.0 %fusion.40 = f32[16,32,640]{2,1,0:T(8,128)S(1)} fusion(f32[16,230]{1,0:T(8,128)S(1)} %get-tuple-element.279, s32[16,230]{1,0:T(8,128)S(1)} %get-tuple-element.280, f32[16,230,32]{1,0,2:T(8,128)S(1)} %broadcast_select_fusion.2), kind=kOutput, calls=%fused_computation.3.clone.1 | convolution fusion | flops 909107200 | bytes 1811200 | tf_op jit(solution)/shard_map/while/body/eval_jaxpr/bea,bep->bap/dot_general | solution.py:44
  86.6 3.7 %fusion.41 = f32[512,640]{1,0:T(8,128)S(1)} fusion(f32[512,640]{1,0:T(8,128)S(1)} %bitcast.27, f32[640,640]{1,0:T(8,128)S(1)} %copy-done), kind=kOutput, calls=%fused_computation.30.clone.1 | convolution fusion | flops 2516582400 | bytes 4259840 | tf_op jit(solution)/shard_map/while/body/eval_jaxpr/dot_general | solution.py:51
  90.6 8.5 %fusion.42 = f32[128,128]{0,1:T(8,128)} fusion(f32[128,128]{0,1:T(8,128)} %get-tuple-element.296, s32[]{:T(128)S(6)} %select_n.60, f32[16,20480]{1,0:T(8,128)S(1)} %reshape.132, f32[20480,128]{1,0:T(8,128)} %get-tuple-element.314), kind=kOutput, calls=%fused_computation.9.clone.1 | convolution fusion | flops 503316480 | bytes 11804676 | tf_op jit(solution)/shard_map/while/body/eval_jaxpr/bm,mi->ib/dot_general | solution.py:57
  99.3 6.3 %gather_fusion = f32[3680,32]{1,0:T(8,128)S(1)} fusion(f32[1024,32]{1,0:T(8,128)S(1)} %get-tuple-element.310, s32[4096]{0:T(1024)S(1)} %pad_clamp_fusion.2), kind=kCustom, calls=%fused_computation.clone.clone.1 | custom fusion | bytes 956800 | tf_op jit(solution)/shard_map/while/body/eval_jaxpr/jit(_take)/gather | solution.py:38
  107.1 8.0 %fusion.40 = f32[16,32,640]{2,1,0:T(8,128)S(1)} fusion(f32[16,230]{1,0:T(8,128)S(1)} %get-tuple-element.279, s32[16,230]{1,0:T(8,128)S(1)} %get-tuple-element.280, f32[16,230,32]{1,0,2:T(8,128)S(1)} %broadcast_select_fusion.2), kind=kOutput, calls=%fused_computation.3.clone.1 | convolution fusion | flops 909107200 | bytes 1811200 | tf_op jit(solution)/shard_map/while/body/eval_jaxpr/bea,bep->bap/dot_general | solution.py:44
  115.0 3.7 %fusion.41 = f32[512,640]{1,0:T(8,128)S(1)} fusion(f32[512,640]{1,0:T(8,128)S(1)} %bitcast.27, f32[640,640]{1,0:T(8,128)S(1)} %copy-done), kind=kOutput, calls=%fused_computation.30.clone.1 | convolution fusion | flops 2516582400 | bytes 4259840 | tf_op jit(solution)/shard_map/while/body/eval_jaxpr/dot_general | solution.py:51
  119.0 8.5 %fusion.42 = f32[128,128]{0,1:T(8,128)} fusion(f32[128,128]{0,1:T(8,128)} %get-tuple-element.296, s32[]{:T(128)S(6)} %select_n.60, f32[16,20480]{1,0:T(8,128)S(1)} %reshape.132, f32[20480,128]{1,0:T(8,128)} %get-tuple-element.314), kind=kOutput, calls=%fused_computation.9.clone.1 | convolution fusion | flops 503316480 | bytes 11804676 | tf_op jit(solution)/shard_map/while/body/eval_jaxpr/bm,mi->ib/dot_general | solution.py:57
  127.7 6.3 %gather_fusion = f32[3680,32]{1,0:T(8,128)S(1)} fusion(f32[1024,32]{1,0:T(8,128)S(1)} %get-tuple-element.310, s32[4096]{0:T(1024)S(1)} %pad_clamp_fusion.2), kind=kCustom, calls=%fused_computation.clone.clone.1 | custom fusion | bytes 956800 | tf_op jit(solution)/shard_map/while/body/eval_jaxpr/jit(_take)/gather | solution.py:38
  135.4 8.0 %fusion.40 = f32[16,32,640]{2,1,0:T(8,128)S(1)} fusion(f32[16,230]{1,0:T(8,128)S(1)} %get-tuple-element.279, s32[16,230]{1,0:T(8,128)S(1)} %get-tuple-element.280, f32[16,230,32]{1,0,2:T(8,128)S(1)} %broadcast_select_fusion.2), kind=kOutput, calls=%fused_computation.3.clone.1 | convolution fusion | flops 909107200 | bytes 1811200 | tf_op jit(solution)/shard_map/while/body/eval_jaxpr/bea,bep->bap/dot_general | solution.py:44
  143.4 3.7 %fusion.41 = f32[512,640]{1,0:T(8,128)S(1)} fusion(f32[512,640]{1,0:T(8,128)S(1)} %bitcast.27, f32[640,640]{1,0:T(8,128)S(1)} %copy-done), kind=kOutput, calls=%fused_computation.30.clone.1 | convolution fusion | flops 2516582400 | bytes 4259840 | tf_op jit(solution)/shard_map/while/body/eval_jaxpr/dot_general | solution.py:51
  147.4 8.5 %fusion.42 = f32[128,128]{0,1:T(8,128)} fusion(f32[128,128]{0,1:T(8,128)} %get-tuple-element.296, s32[]{:T(128)S(6)} %select_n.60, f32[16,20480]{1,0:T(8,128)S(1)} %reshape.132, f32[20480,128]{1,0:T(8,128)} %get-tuple-element.314), kind=kOutput, calls=%fused_computation.9.clone.1 | convolution fusion | flops 503316480 | bytes 11804676 | tf_op jit(solution)/shard_map/while/body/eval_jaxpr/bm,mi->ib/dot_general | solution.py:57
  156.1 6.3 %gather_fusion = f32[3680,32]{1,0:T(8,128)S(1)} fusion(f32[1024,32]{1,0:T(8,128)S(1)} %get-tuple-element.310, s32[4096]{0:T(1024)S(1)} %pad_clamp_fusion.2), kind=kCustom, calls=%fused_computation.clone.clone.1 | custom fusion | bytes 956800 | tf_op jit(solution)/shard_map/while/body/eval_jaxpr/jit(_take)/gather | solution.py:38
  163.8 8.0 %fusion.40 = f32[16,32,640]{2,1,0:T(8,128)S(1)} fusion(f32[16,230]{1,0:T(8,128)S(1)} %get-tuple-element.279, s32[16,230]{1,0:T(8,128)S(1)} %get-tuple-element.280, f32[16,230,32]{1,0,2:T(8,128)S(1)} %broadcast_select_fusion.2), kind=kOutput, calls=%fused_computation.3.clone.1 | convolution fusion | flops 909107200 | bytes 1811200 | tf_op jit(solution)/shard_map/while/body/eval_jaxpr/bea,bep->bap/dot_general | solution.py:44
  175.8 8.5 %fusion.42 = f32[128,128]{0,1:T(8,128)} fusion(f32[128,128]{0,1:T(8,128)} %get-tuple-element.296, s32[]{:T(128)S(6)} %select_n.60, f32[16,20480]{1,0:T(8,128)S(1)} %reshape.132, f32[20480,128]{1,0:T(8,128)} %get-tuple-element.314), kind=kOutput, calls=%fused_computation.9.clone.1 | convolution fusion | flops 503316480 | bytes 11804676 | tf_op jit(solution)/shard_map/while/body/eval_jaxpr/bm,mi->ib/dot_general | solution.py:57
  184.5 6.3 %gather_fusion = f32[3680,32]{1,0:T(8,128)S(1)} fusion(f32[1024,32]{1,0:T(8,128)S(1)} %get-tuple-element.310, s32[4096]{0:T(1024)S(1)} %pad_clamp_fusion.2), kind=kCustom, calls=%fused_computation.clone.clone.1 | custom fusion | bytes 956800 | tf_op jit(solution)/shard_map/while/body/eval_jaxpr/jit(_take)/gather | solution.py:38
  192.2 8.0 %fusion.40 = f32[16,32,640]{2,1,0:T(8,128)S(1)} fusion(f32[16,230]{1,0:T(8,128)S(1)} %get-tuple-element.279, s32[16,230]{1,0:T(8,128)S(1)} %get-tuple-element.280, f32[16,230,32]{1,0,2:T(8,128)S(1)} %broadcast_select_fusion.2), kind=kOutput, calls=%fused_computation.3.clone.1 | convolution fusion | flops 909107200 | bytes 1811200 | tf_op jit(solution)/shard_map/while/body/eval_jaxpr/bea,bep->bap/dot_general | solution.py:44
  204.2 8.5 %fusion.42 = f32[128,128]{0,1:T(8,128)} fusion(f32[128,128]{0,1:T(8,128)} %get-tuple-element.296, s32[]{:T(128)S(6)} %select_n.60, f32[16,20480]{1,0:T(8,128)S(1)} %reshape.132, f32[20480,128]{1,0:T(8,128)} %get-tuple-element.314), kind=kOutput, calls=%fused_computation.9.clone.1 | convolution fusion | flops 503316480 | bytes 11804676 | tf_op jit(solution)/shard_map/while/body/eval_jaxpr/bm,mi->ib/dot_general | solution.py:57
  212.9 6.3 %gather_fusion = f32[3680,32]{1,0:T(8,128)S(1)} fusion(f32[1024,32]{1,0:T(8,128)S(1)} %get-tuple-element.310, s32[4096]{0:T(1024)S(1)} %pad_clamp_fusion.2), kind=kCustom, calls=%fused_computation.clone.clone.1 | custom fusion | bytes 956800 | tf_op jit(solution)/shard_map/while/body/eval_jaxpr/jit(_take)/gather | solution.py:38
  220.6 8.0 %fusion.40 = f32[16,32,640]{2,1,0:T(8,128)S(1)} fusion(f32[16,230]{1,0:T(8,128)S(1)} %get-tuple-element.279, s32[16,230]{1,0:T(8,128)S(1)} %get-tuple-element.280, f32[16,230,32]{1,0,2:T(8,128)S(1)} %broadcast_select_fusion.2), kind=kOutput, calls=%fused_computation.3.clone.1 | convolution fusion | flops 909107200 | bytes 1811200 | tf_op jit(solution)/shard_map/while/body/eval_jaxpr/bea,bep->bap/dot_general | solution.py:44
  228.6 3.7 %fusion.41 = f32[512,640]{1,0:T(8,128)S(1)} fusion(f32[512,640]{1,0:T(8,128)S(1)} %bitcast.27, f32[640,640]{1,0:T(8,128)S(1)} %copy-done), kind=kOutput, calls=%fused_computation.30.clone.1 | convolution fusion | flops 2516582400 | bytes 4259840 | tf_op jit(solution)/shard_map/while/body/eval_jaxpr/dot_general | solution.py:51
  232.6 8.5 %fusion.42 = f32[128,128]{0,1:T(8,128)} fusion(f32[128,128]{0,1:T(8,128)} %get-tuple-element.296, s32[]{:T(128)S(6)} %select_n.60, f32[16,20480]{1,0:T(8,128)S(1)} %reshape.132, f32[20480,128]{1,0:T(8,128)} %get-tuple-element.314), kind=kOutput, calls=%fused_computation.9.clone.1 | convolution fusion | flops 503316480 | bytes 11804676 | tf_op jit(solution)/shard_map/while/body/eval_jaxpr/bm,mi->ib/dot_general | solution.py:57
  241.3 6.3 %gather_fusion = f32[3680,32]{1,0:T(8,128)S(1)} fusion(f32[1024,32]{1,0:T(8,128)S(1)} %get-tuple-element.310, s32[4096]{0:T(1024)S(1)} %pad_clamp_fusion.2), kind=kCustom, calls=%fused_computation.clone.clone.1 | custom fusion | bytes 956800 | tf_op jit(solution)/shard_map/while/body/eval_jaxpr/jit(_take)/gather | solution.py:38
  249.0 8.0 %fusion.40 = f32[16,32,640]{2,1,0:T(8,128)S(1)} fusion(f32[16,230]{1,0:T(8,128)S(1)} %get-tuple-element.279, s32[16,230]{1,0:T(8,128)S(1)} %get-tuple-element.280, f32[16,230,32]{1,0,2:T(8,128)S(1)} %broadcast_select_fusion.2), kind=kOutput, calls=%fused_computation.3.clone.1 | convolution fusion | flops 909107200 | bytes 1811200 | tf_op jit(solution)/shard_map/while/body/eval_jaxpr/bea,bep->bap/dot_general | solution.py:44
  261.0 8.5 %fusion.42 = f32[128,128]{0,1:T(8,128)} fusion(f32[128,128]{0,1:T(8,128)} %get-tuple-element.296, s32[]{:T(128)S(6)} %select_n.60, f32[16,20480]{1,0:T(8,128)S(1)} %reshape.132, f32[20480,128]{1,0:T(8,128)} %get-tuple-element.314), kind=kOutput, calls=%fused_computation.9.clone.1 | convolution fusion | flops 503316480 | bytes 11804676 | tf_op jit(solution)/shard_map/while/body/eval_jaxpr/bm,mi->ib/dot_general | solution.py:57
  269.7 6.3 %gather_fusion = f32[3680,32]{1,0:T(8,128)S(1)} fusion(f32[1024,32]{1,0:T(8,128)S(1)} %get-tuple-element.310, s32[4096]{0:T(1024)S(1)} %pad_clamp_fusion.2), kind=kCustom, calls=%fused_computation.clone.clone.1 | custom fusion | bytes 956800 | tf_op jit(solution)/shard_map/while/body/eval_jaxpr/jit(_take)/gather | solution.py:38
  277.4 8.0 %fusion.40 = f32[16,32,640]{2,1,0:T(8,128)S(1)} fusion(f32[16,230]{1,0:T(8,128)S(1)} %get-tuple-element.279, s32[16,230]{1,0:T(8,128)S(1)} %get-tuple-element.280, f32[16,230,32]{1,0,2:T(8,128)S(1)} %broadcast_select_fusion.2), kind=kOutput, calls=%fused_computation.3.clone.1 | convolution fusion | flops 909107200 | bytes 1811200 | tf_op jit(solution)/shard_map/while/body/eval_jaxpr/bea,bep->bap/dot_general | solution.py:44
  289.3 8.5 %fusion.42 = f32[128,128]{0,1:T(8,128)} fusion(f32[128,128]{0,1:T(8,128)} %get-tuple-element.296, s32[]{:T(128)S(6)} %select_n.60, f32[16,20480]{1,0:T(8,128)S(1)} %reshape.132, f32[20480,128]{1,0:T(8,128)} %get-tuple-element.314), kind=kOutput, calls=%fused_computation.9.clone.1 | convolution fusion | flops 503316480 | bytes 11804676 | tf_op jit(solution)/shard_map/while/body/eval_jaxpr/bm,mi->ib/dot_general | solution.py:57
  299.4 20.8 %reduce-scatter.2.cloned.1.call-done = f32[32,128]{1,0:T(8,128)} async-done(((f32[128,128]{1,0:T(8,128)}), f32[32,128]{1,0:T(8,128)}) %reduce-scatter.2.cloned.1.call-update) | async-done | bytes 16400 | tf_op jit(solution)/shard_map/reduce_scatter | solution.py:72
  (108 shorter events, 37.3 us)
Async XLA Ops:
  6.5 37.7 %copy-start.1 = (f32[528,528]{1,0:T(8,128)S(1)}, f32[528,528]{1,0:T(8,128)}, u32[]{:S(2)}) copy-start(f32[528,528]{1,0:T(8,128)} %param.13) | copy-start | bytes 3345412
  6.5 39.0 %copy-start.3 = (s32[32,230]{1,0:T(8,128)S(1)}, s32[32,230]{1,0:T(8,128)}, u32[]{:S(2)}) copy-start(s32[32,230]{1,0:T(8,128)} %param.18) | copy-start | bytes 88324
  6.5 39.0 %copy-start.2 = (s32[32,230]{1,0:T(8,128)S(1)}, s32[32,230]{1,0:T(8,128)}, u32[]{:S(2)}) copy-start(s32[32,230]{1,0:T(8,128)} %param.17) | copy-start | bytes 88324
  6.5 313.7 %reduce-scatter.2.cloned.1.call-start = ((), (), s32[]{:S(2)}) async-start(), calls=%async_computation.1 | async-start | bytes 81920 | tf_op jit(solution)/shard_map/reduce_scatter | solution.py:72
  78.6 8.0 %copy-start = (f32[640,640]{1,0:T(8,128)S(1)}, f32[640,640]{1,0:T(8,128)}, u32[]{:S(2)}) copy-start(f32[640,640]{1,0:T(8,128)} %get-tuple-element.313) | copy-start | bytes 4915204 | tf_op jit(solution)/shard_map/while
  107.0 8.0 %copy-start = (f32[640,640]{1,0:T(8,128)S(1)}, f32[640,640]{1,0:T(8,128)}, u32[]{:S(2)}) copy-start(f32[640,640]{1,0:T(8,128)} %get-tuple-element.313) | copy-start | bytes 4915204 | tf_op jit(solution)/shard_map/while
  135.4 8.0 %copy-start = (f32[640,640]{1,0:T(8,128)S(1)}, f32[640,640]{1,0:T(8,128)}, u32[]{:S(2)}) copy-start(f32[640,640]{1,0:T(8,128)} %get-tuple-element.313) | copy-start | bytes 4915204 | tf_op jit(solution)/shard_map/while
  163.8 8.0 %copy-start = (f32[640,640]{1,0:T(8,128)S(1)}, f32[640,640]{1,0:T(8,128)}, u32[]{:S(2)}) copy-start(f32[640,640]{1,0:T(8,128)} %get-tuple-element.313) | copy-start | bytes 4915204 | tf_op jit(solution)/shard_map/while
  192.2 8.0 %copy-start = (f32[640,640]{1,0:T(8,128)S(1)}, f32[640,640]{1,0:T(8,128)}, u32[]{:S(2)}) copy-start(f32[640,640]{1,0:T(8,128)} %get-tuple-element.313) | copy-start | bytes 4915204 | tf_op jit(solution)/shard_map/while
  220.6 8.0 %copy-start = (f32[640,640]{1,0:T(8,128)S(1)}, f32[640,640]{1,0:T(8,128)}, u32[]{:S(2)}) copy-start(f32[640,640]{1,0:T(8,128)} %get-tuple-element.313) | copy-start | bytes 4915204 | tf_op jit(solution)/shard_map/while
  249.0 8.0 %copy-start = (f32[640,640]{1,0:T(8,128)S(1)}, f32[640,640]{1,0:T(8,128)}, u32[]{:S(2)}) copy-start(f32[640,640]{1,0:T(8,128)} %get-tuple-element.313) | copy-start | bytes 4915204 | tf_op jit(solution)/shard_map/while
  277.4 8.0 %copy-start = (f32[640,640]{1,0:T(8,128)S(1)}, f32[640,640]{1,0:T(8,128)}, u32[]{:S(2)}) copy-start(f32[640,640]{1,0:T(8,128)} %get-tuple-element.313) | copy-start | bytes 4915204 | tf_op jit(solution)/shard_map/while
Sparse Core Ops, SparseCore 0:
  299.5 20.6 reduce-scatter.1
where the time goes:
time: 327 us
  matrix products  186 us (57%)
  local copies, waits for them, and re-layouts  71.4 us (22%)
  blocking collectives  33 us (10%)
  waiting for transfers between devices  20.8 us (6%)
  between operations  13.4 us (4%)
    dot_general x8, matrix products, block_terms(): jnp.einsum('bm,mi->ib', mixed, fold, precision=lax.Precision.HIGHEST, pre...  67.8 us
    dot_general x8, matrix products, block_terms(): jnp.einsum('bea,bep->bap', values, beta_onehot, precision=lax.Precision.H...  63.9 us
    gather x24, local copies, waits for them, and re-layouts, block_terms(): jnp.take(by_column, targets.reshape(-1), axis=0)  61.2 us
    all_gather x1, blocking collectives, local(): gathered = lax.all_gather(coeff, 'beta', axis=1, tiled=True)  33 us
    dot_general x8, matrix products, block_terms(): jnp.dot(lifted.reshape(-1, width), padded_ints, precision=lax.Precision.H...  29.7 us
    dot_general x1, matrix products, local(): jnp.einsum('aeq,aei->aqi', alpha_onehot, target_onehot, precision=lax.Pre...  24.5 us
    reduce_scatter x1, waiting for transfers between devices, local(): lax.psum_scatter(partial_value, 'alpha', scatter_dimension=0, tiled=True)  20.8 us
  transfers between devices with their start and end apart: 1, of which 1 were waited for; matrix products, arithmetic and copies ran while one was open for 0% of the time, Pallas kernels for 0%

commit v1 on v0

v1 whole, which is shorter than its diff:
```python
import functools

import jax
import jax.numpy as jnp
from jax import lax
from jax.experimental import pallas as pl
from jax.experimental.pallas import tpu as pltpu
from jax.sharding import PartitionSpec as P

BF = jnp.bfloat16
F32 = jnp.float32
I32 = jnp.int32
NT = (((1,), (1,)), ((), ()))


def split(x):
    hi = x.astype(BF)
    return hi, (x - hi.astype(F32)).astype(BF)


def fold_kernel(rows,pairs_ref,tg_ref,sg_ref,v_ref,g_ref,vcat,wcat,rows_p,rows_t,rows_s):
    n_pairs=v_ref.shape[0]; na=g_ref.shape[2]//2
    main=n_pairs//128*128; rest=n_pairs-main
    exc=pairs_ref.shape[1]; ew=rows_p.shape[0]*128
    @pl.when(pl.program_id(0)==0)
    def _():
        hi,lo=split(v_ref[...])
        vcat[:,:main]=hi[:,:main]; vcat[:,main:2*main]=lo[:,:main]
        vcat[:,2*main:2*main+rest]=hi[:,main:]; vcat[:,2*main+rest:2*main+2*rest]=lo[:,main:]
    def row(ref,j,fill):
        r=ref[j:j+1,:]
        return r
    for jp in range(rows//2):
        for h in range(2):
            j=2*jp+h
            pr=pairs_ref[j:j+1,:]; tr=tg_ref[j:j+1,:]; sr=sg_ref[j:j+1,:].astype(F32)
            op=jnp.where(lax.broadcasted_iota(jnp.int32,(n_pairs,exc),0)==pr,1.0,0.0).astype(BF)
            tt=jnp.where(lax.broadcasted_iota(jnp.int32,(na,exc),0)==tr,sr,0.0).astype(BF)
            w=lax.dot_general(op,tt,NT,preferred_element_type=F32).astype(BF)
            c=slice(h*na,(h+1)*na)
            s=jp%2
            wcat[s,0:main,c]=w[:main]; wcat[s,main:2*main,c]=w[:main]
            wcat[s,2*main:2*main+rest,c]=w[main:]; wcat[s,2*main+rest:2*main+2*rest,c]=w[main:]
        g=jnp.dot(vcat[...],wcat[jp%2],preferred_element_type=F32)
        for h in range(2):
            j=2*jp+h
            hi,lo=split(g[:,h*na:(h+1)*na])
            g_ref[j,:n_pairs,:na]=hi; g_ref[j,:n_pairs,na:]=lo
            g_ref[j,n_pairs:,:]=jnp.zeros((g_ref.shape[1]-n_pairs,2*na),BF)
def fold(pairs,tg,sg,v,total_rows):
    rows_here,exc=pairs.shape; n_pairs=v.shape[0]; w=(n_pairs+127)//128*128
    rows=8; ew=(exc+127)//128
    main=n_pairs//128*128; rest=n_pairs-main
    kc=2*n_pairs
    tab=pl.BlockSpec((rows,exc),lambda i:(i,0))
    return pl.pallas_call(functools.partial(fold_kernel,rows),
        out_shape=jax.ShapeDtypeStruct((rows_here,w,2*total_rows),BF),
        grid=(rows_here//rows,),
        in_specs=[tab,tab,tab,pl.BlockSpec((n_pairs,n_pairs),lambda i:(0,0))],
        out_specs=pl.BlockSpec((rows,w,2*total_rows),lambda i:(i,0,0)),
        scratch_shapes=[pltpu.VMEM((n_pairs,kc),BF),pltpu.VMEM((2,kc,2*total_rows),BF),
           pltpu.VMEM((ew,rows_here,128),jnp.int32),pltpu.VMEM((ew,rows_here,128),jnp.int32),pltpu.VMEM((ew,rows_here,128),F32)],
    )(pairs,tg,sg,v)
def gath(x,idx): return jnp.take_along_axis(x,idx,axis=1,mode="promise_in_bounds")
def inv_kernel(chunks,pairs_ref,inv_ref,scr):
    nb,exc=pairs_ref.shape
    last=inv_ref.shape[1]
    ew=(exc+128)//128*128
    def body(g,_):
        b0=pl.multiple_of(g*8,8)
        pr8=pairs_ref[pl.ds(b0,8),:]
        for h in range(4):
            os_=[];xs=[]
            for j in (2*h,2*h+1):
                pr=pr8[j:j+1,:]
                lane=pr&127; ch=pr>>7
                os_.append(jnp.where(lax.broadcasted_iota(I32,(128,exc),0)==lane,1.0,0.0).astype(BF))
                code=(lax.broadcasted_iota(I32,(8,exc),1)-(ew-1)).astype(F32)
                xs.append(jnp.where(lax.broadcasted_iota(I32,(8,exc),0)==ch,code,0.0))
            o=jnp.concatenate(os_,0); x=jnp.concatenate(xs,0).astype(BF)
            r=lax.dot_general(x,o,NT,preferred_element_type=F32)
            for q,j in enumerate((2*h,2*h+1)):
                scr[pl.ds(b0+j,8,stride=nb),:]=r[q*8:(q+1)*8,q*128:(q+1)*128]
        return 0
    lax.fori_loop(0,nb//8,body,0)
    for c in range(chunks):
        inv_ref[c]=scr[c*nb:(c+1)*nb,:].astype(I32)+(ew-1)
def inverse(pairs,n_pairs):
    nb,exc=pairs.shape; chunks=(n_pairs+127)//128
    return pl.pallas_call(functools.partial(inv_kernel,chunks),
       out_shape=jax.ShapeDtypeStruct((chunks,nb,128),I32),
       in_specs=[pl.BlockSpec(memory_space=pltpu.VMEM)],out_specs=pl.BlockSpec(memory_space=pltpu.VMEM),
       scratch_shapes=[pltpu.VMEM((8*nb,128),F32)])(pairs)
def tree(parts,masks):
    lvl=0
    while len(parts)>1:
        parts=[jnp.where(masks[lvl],parts[2*i+1],parts[2*i]) for i in range(len(parts)//2)]; lvl+=1
    return parts[0]
def sig_kernel(c_ref,tg_ref,sg_ref,inv_ref,g_hbm,o_ref,tgs,sgs,vals,lift,gv,sem):
    nk,na,lanes=c_ref.shape
    nb,exc=tg_ref.shape
    ew=tgs.shape[1]; chunks=inv_ref.shape[0]; ni=g_hbm.shape[2]//2
    cp=pltpu.make_async_copy(g_hbm,gv,sem); cp.start()
    tgs[:,:exc]=tg_ref[...]; tgs[:,exc:]=jnp.zeros((nb,ew-exc),I32)
    sgs[:,:exc]=sg_ref[...].astype(F32); sgs[:,exc:]=jnp.zeros((nb,ew-exc),F32)
    bits=nk.bit_length()-1
    def gbody(g,_):
        bs=pl.multiple_of(g*8,8)
        for ec in range(ew//128):
            t=tgs[pl.ds(bs,8),ec*128:(ec+1)*128]; s=sgs[pl.ds(bs,8),ec*128:(ec+1)*128]
            lane=t&127; ch=t>>7
            ms=[(ch&(1<<i))!=0 for i in range(bits)]
            def one(a,_):
                v=tree([gath(c_ref[k,pl.ds(a,8,stride=0),:],lane) for k in range(nk)],ms)*s
                vals[a,pl.ds(bs,8),ec*128:(ec+1)*128]=v
                return 0
            lax.fori_loop(0,na,one,0,unroll=True)
        return 0
    lax.fori_loop(0,nb//8,gbody,0)
    def lbody(g,_):
        b0=pl.multiple_of(g*16,16)
        for pc in range(chunks):
            idx=[inv_ref[pc,pl.ds(pl.multiple_of(b0+8*h,8),8),:] for h in range(2)]
            ln=[i&127 for i in idx]
            ms=[[((i>>7)&(1<<q))!=0 for q in range((ew//128-1).bit_length())] for i in idx]
            def one(a,_):
                x=jnp.concatenate([tree([gath(vals[a,pl.ds(pl.multiple_of(b0+8*h,8),8),ec*128:(ec+1)*128],ln[h]) for ec in range(ew//128)],ms[h]) for h in range(2)],0)
                hi,lo=split(x)
                lift[a,pl.ds(b0,16),pc*128:(pc+1)*128]=hi
                lift[a,pl.ds(nb+b0,16),pc*128:(pc+1)*128]=lo
                return 0
            lax.fori_loop(0,na,one,0,unroll=True)
        return 0
    lax.fori_loop(0,nb//16,lbody,0)
    cp.wait()
    def mm(ap,acc):
        for j in range(2):
            acc=acc+jnp.dot(lift[2*ap+j],gv[2*ap+j],preferred_element_type=F32)
        return acc
    acc=lax.fori_loop(0,na//2,mm,jnp.zeros((2*nb,2*ni),F32))
    tot=(acc[:nb,:ni]+acc[nb:,:ni])+(acc[:nb,ni:]+acc[nb:,ni:])
    o_ref[...]=tot.T
def sig(c,tg,sg,inv,g):
    nk,na,lanes=c.shape; nb,exc=tg.shape; chunks=inv.shape[0]; ni=g.shape[2]//2
    ew=(exc+128)//128*128
    vm=pl.BlockSpec(memory_space=pltpu.VMEM)
    return pl.pallas_call(sig_kernel,out_shape=jax.ShapeDtypeStruct((ni,nb),F32),
       in_specs=[vm]*4+[pl.BlockSpec(memory_space=pl.ANY)],out_specs=vm,
       scratch_shapes=[pltpu.VMEM((nb,ew),I32),pltpu.VMEM((nb,ew),F32),pltpu.VMEM((na,nb,ew),F32),
          pltpu.VMEM((na,2*nb,chunks*128),BF),pltpu.VMEM(g.shape,BF),pltpu.SemaphoreType.DMA(())])(c,tg,sg,inv,g)

def local(
    coeff, integrals, beta_pairs, beta_targets, beta_signs, alpha_pairs, alpha_targets, alpha_signs
):
    n_beta = lax.axis_size("beta")
    n_alpha = lax.axis_size("alpha")
    rows, cols = coeff.shape
    n_pairs = integrals.shape[0]
    table = coeff[None]
    step = 1
    while step < n_beta:
        other = lax.ppermute(table, "beta", [(i, i ^ step) for i in range(n_beta)])
        table = jnp.concatenate([table, other], 0)
        step *= 2
    me = lax.axis_index("beta")
    targets = beta_targets ^ (me * cols)
    g = fold(alpha_pairs, alpha_targets, alpha_signs, integrals, rows * n_alpha)
    inv = inverse(beta_pairs, n_pairs)
    partial = sig(table, targets, beta_signs, inv, g)
    parts = partial.reshape(n_alpha, rows, cols)
    mine = lax.axis_index("alpha")
    total = lax.dynamic_index_in_dim(parts, mine, 0, False)
    for k in range(1, n_alpha):
        block = lax.dynamic_index_in_dim(parts, mine ^ k, 0, False)
        total = total + lax.ppermute(block, "alpha", [(i, i ^ k) for i in range(n_alpha)])
    return total


def solution(mesh):
    placed = (
        P("alpha", "beta"),
        P(),
        P("beta", None),
        P("beta", None),
        P("beta", None),
        P("alpha", None),
        P("alpha", None),
        P("alpha", None),
    )
    return jax.shard_map(
        local, mesh=mesh, in_specs=placed, out_specs=P("alpha", "beta"), check_vma=False
    )
```

time: 327 us -> 75.4 us (0.23)
  matrix products: 186 us -> 0 us
  local copies, waits for them, and re-layouts: 71.4 us -> 5.05 us
  Pallas kernels: 0 us -> 49.9 us
  blocking collectives: 33 us -> 0 us
  waiting for transfers between devices: 20.8 us -> 5.75 us
  between operations: 13.4 us -> 0.04 us
  starting transfers between devices: 0.01 us -> 9.9 us
    dot_general x25 -> x0, matrix products: 186 us -> none  [the longest x8 67.8 us: block_terms(): jnp.einsum('bm,mi->ib', mixed, fold, precision=lax.Precision.HIGHEST, pre...]
    gather x24 -> x0, local copies, waits for them, and re-layouts: 61.2 us -> none  [block_terms(): jnp.take(by_column, targets.reshape(-1), axis=0)]
    pallas_call x0 -> x3, Pallas kernels: none -> 49.9 us  [the longest x1 30.5 us: sig(): pl.pallas_call(sig_kernel, out_shape=jax.ShapeDtypeStruct((ni, nb), F32),...]
    all_gather x1 -> x0, blocking collectives: 33 us -> none  [local(): gathered = lax.all_gather(coeff, 'beta', axis=1, tiled=True)]
    reduce_scatter x1 -> x0, waiting for transfers between devices: 20.8 us -> none  [local(): lax.psum_scatter(partial_value, 'alpha', scatter_dimension=0, tiled=True)]
    ppermute x0 -> x6, starting transfers between devices: none -> 9.9 us  [the longest x3 8.04 us: local(): other = lax.ppermute(table, 'beta', [(i, i ^ step) for i in range(n_beta)])]
    ppermute x0 -> x6, waiting for transfers between devices: none -> 5.75 us  [the longest x3 2.89 us: local(): other = lax.ppermute(table, 'beta', [(i, i ^ step) for i in range(n_beta)])]
  transfers between devices with their start and end apart: 1 -> 6, of which waited for: 1 -> 4; matrix products, arithmetic and copies ran while one was open for 0% -> 7% of each run, Pallas kernels for 0% -> 26%
where the time goes in v1:
time: 75.4 us; the launch traced here: 74.7 us
  Pallas kernels  49.9 us (66%)
  starting transfers between devices  9.9 us (13%)
  waiting for transfers between devices  5.75 us (8%)
  local copies, waits for them, and re-layouts  5.05 us (7%)
  other arithmetic  4.1 us (5%)
    pallas_call x1, Pallas kernels, sig(): pl.pallas_call(sig_kernel, out_shape=jax.ShapeDtypeStruct((ni, nb), F32),...  30.5 us
    pallas_call x1, Pallas kernels, fold(): pl.pallas_call(functools.partial(fold_kernel, rows), out_shape=jax.ShapeD...  13.5 us
    ppermute x3, starting transfers between devices, local(): other = lax.ppermute(table, 'beta', [(i, i ^ step) for i in range(n_beta)])  8.04 us
    pallas_call x1, Pallas kernels, inverse(): pl.pallas_call(functools.partial(inv_kernel, chunks), out_shape=jax.Shape...  5.88 us
    unnamed x5, local copies, waits for them, and re-layouts  4.28 us
    ppermute x3, waiting for transfers between devices, local(): other = lax.ppermute(table, 'beta', [(i, i ^ step) for i in range(n_beta)])  2.89 us
    ppermute x3, waiting for transfers between devices, local(): lax.ppermute(block, 'alpha', [(i, i ^ k) for i in range(n_alpha)])  2.87 us
    concatenate x3, other arithmetic, local(): table = jnp.concatenate([table, other], 0)  2.12 us
  transfers between devices with their start and end apart: 6, of which 4 were waited for; matrix products, arithmetic and copies ran while one was open for 7% of the time, Pallas kernels for 26%

profile of v1, /device:TPU:0, one launch (start us, length us, event | category | flops | bytes accessed | tf_op | source)
XLA Modules:
  0.0 74.7 jit_solution(2896679298151885382)
XLA Ops:
  0.0 0.0 copy-start
  0.0 3.0 %collective-permute-start = (f32[1,32,128]{2,1,0:T(8,128)}, f32[1,32,128]{2,1,0:T(8,128)S(1)}, u32[]{:S(2)}, u32[]{:S(2)}) collective-permute-start(f32[1,32,128]{2,1,0:T(8,128)} %bitcast.16), channel_id=1, source_target_pairs={{0,1},{1,0},{2,3},{3,2},{4,5},{5,4},{6,7},{7,6},{8,9},{9,8},{10,11... | collective-permute-start | bytes 49160 | tf_op jit(solution)/shard_map/ppermute | solution.py:162
  3.0 2.0 %collective-permute-done = f32[1,32,128]{2,1,0:T(8,128)S(1)} collective-permute-done((f32[1,32,128]{2,1,0:T(8,128)}, f32[1,32,128]{2,1,0:T(8,128)S(1)}, u32[]{:S(2)}, u32[]{:S(2)}) %collective-permute-start) | collective-permute-done | bytes 16416 | tf_op jit(solution)/shard_map/ppermute | solution.py:162
  5.0 0.7 pad_maximum_fusion.2
  5.7 2.0 %collective-permute-start.1 = (f32[2,32,128]{2,1,0:T(8,128)S(1)}, f32[2,32,128]{2,1,0:T(8,128)S(1)}, u32[]{:S(2)}, u32[]{:S(2)}) collective-permute-start(f32[2,32,128]{2,1,0:T(8,128)S(1)} %pad_maximum_fusion.2), channel_id=1, source_target_pairs={{0,2},{1,3},{2,0},{3,1},{4,6},{5,7},{6,4},{7,5},{8,10},{9,11},{10,... | collective-permute-start | bytes 98312 | tf_op jit(solution)/shard_map/ppermute | solution.py:162
  7.7 1.0 %copy.12 = s32[128,230]{1,0:T(8,128)S(1)} copy(s32[128,230]{0,1:T(8,128)} %param.11) | data formatting | bytes 235520 | tf_op args[3]
  8.7 0.9 %collective-permute-done.1 = f32[2,32,128]{2,1,0:T(8,128)S(1)} collective-permute-done((f32[2,32,128]{2,1,0:T(8,128)S(1)}, f32[2,32,128]{2,1,0:T(8,128)S(1)}, u32[]{:S(2)}, u32[]{:S(2)}) %collective-permute-start.1) | collective-permute-done | bytes 32800 | tf_op jit(solution)/shard_map/ppermute | solution.py:162
  9.6 0.7 pad_maximum_fusion.1
  10.3 3.0 %collective-permute-start.2 = (f32[4,32,128]{2,1,0:T(8,128)S(1)}, f32[4,32,128]{2,1,0:T(8,128)S(1)}, u32[]{:S(2)}, u32[]{:S(2)}) collective-permute-start(f32[4,32,128]{2,1,0:T(8,128)S(1)} %pad_maximum_fusion.1), channel_id=1, source_target_pairs={{0,4},{1,5},{2,6},{3,7},{4,0},{5,1},{6,2},{7,3},{8,12},{9,13},{10,... | collective-permute-start | bytes 196616 | tf_op jit(solution)/shard_map/ppermute | solution.py:162
  13.4 0.7 broadcast_xor_fusion.tg_ref
  14.0 1.7 %copy.14.pairs_ref = s32[128,230]{1,0:T(8,128)} copy(s32[128,230]{0,1:T(8,128)} %param.10) | data formatting | bytes 235520 | tf_op args[2]
  15.7 5.9 %shard_map.82.inv_ref = s32[5,128,128]{2,1,0:T(8,128)} custom-call(s32[128,230]{1,0:T(8,128)} %copy.14.pairs_ref), custom_call_target="tpu_custom_call" | custom-call | tf_op jit(solution)/shard_map/pallas_call | solution.py:90
  21.6 1.6 %copy.15.sg_ref = s32[128,230]{1,0:T(8,128)} copy(s32[128,230]{0,1:T(8,128)} %param.12) | data formatting | bytes 235520 | tf_op args[4]
  23.2 13.5 %shard_map.83.g_hbm = bf16[32,640,256]{2,1,0:T(8,128)(2,1)} custom-call(s32[32,230]{1,0:T(8,128)} %pairs_ref.2, s32[32,230]{1,0:T(8,128)} %tg_ref.1, s32[32,230]{1,0:T(8,128)} %sg_ref.2, f32[528,528]{1,0:T(8,128)} %v_ref.1), custom_call_target="tpu_custom_call" | custom-call | tf_op jit(solution)/shard_map/pallas_call | solution.py:56
  36.7 0.0 collective-permute-done.2
  36.7 0.0 copy-done
  36.7 0.7 pad_maximum_fusion.c_ref
  37.4 30.5 %shard_map.84 = f32[128,128]{1,0:T(8,128)} custom-call(f32[8,32,128]{2,1,0:T(8,128)} %pad_maximum_fusion.c_ref, s32[128,230]{1,0:T(8,128)} %broadcast_xor_fusion.tg_ref, s32[128,230]{1,0:T(8,128)} %copy.15.sg_ref, s32[5,128,128]{2,1,0:T(8,128)} %shard_map.82.inv_ref, bf16[32,640,256]{2,1,0:T(8,128)(2,1)} %shard_map.83.g_hbm), custom_call_target="tpu_custom_call" | custom-call | tf_op jit(solution)/shard_map/pallas_call | solution.py:147
  67.9 0.8 %dynamic-slice_bitcast_fusion.2 = (f32[32,128]{1,0:T(8,128)S(1)}, f32[32,128]{1,0:T(8,128)S(1)}, f32[32,128]{1,0:T(8,128)S(1)}) fusion(f32[4,32,128]{2,1,0:T(8,128)} %bitcast.14, s32[]{:T(128)S(6)} %select_n.14, s32[]{:T(128)S(6)} %select_n.16, s32[]{:T(128)S(6)} %select_n.15), kind=kLoop, calls=%fused_computation.9 | loop fusion | bytes 98316 | tf_op jit(solution)/shard_map/jit(dynamic_index_in_dim)/squeeze | solution.py:174
  68.6 0.0 collective-permute-start.3
  68.6 1.6 %collective-permute-start.4 = (f32[32,128]{1,0:T(8,128)S(1)}, f32[32,128]{1,0:T(8,128)S(1)}, u32[]{:S(2)}, u32[]{:S(2)}) collective-permute-start(f32[32,128]{1,0:T(8,128)S(1)} %get-tuple-element.7), channel_id=1, source_target_pairs={{0,16},{8,24},{16,0},{24,8},{1,17},{9,25},{17,1},{25,9},{2,18},{10... | collective-permute-start | bytes 49160 | tf_op jit(solution)/shard_map/ppermute | solution.py:175
  70.2 0.3 collective-permute-start.5
  70.5 0.0 collective-permute-done.3
  70.5 1.9 %collective-permute-done.4 = f32[32,128]{1,0:T(8,128)S(1)} collective-permute-done((f32[32,128]{1,0:T(8,128)S(1)}, f32[32,128]{1,0:T(8,128)S(1)}, u32[]{:S(2)}, u32[]{:S(2)}) %collective-permute-start.4) | collective-permute-done | bytes 16416 | tf_op jit(solution)/shard_map/ppermute | solution.py:175
  72.4 0.9 %collective-permute-done.5 = f32[32,128]{1,0:T(8,128)S(1)} collective-permute-done((f32[32,128]{1,0:T(8,128)S(1)}, f32[32,128]{1,0:T(8,128)S(1)}, u32[]{:S(2)}, u32[]{:S(2)}) %collective-permute-start.5) | collective-permute-done | bytes 16416 | tf_op jit(solution)/shard_map/ppermute | solution.py:175
  73.4 1.3 %fusion.1 = f32[32,128]{1,0:T(8,128)} fusion(f32[32,128]{1,0:T(8,128)S(1)} %collective-permute-done.5, f32[32,128]{1,0:T(8,128)S(1)} %collective-permute-done.4, f32[32,128]{1,0:T(8,128)S(1)} %collective-permute-done.3, f32[4,32,128]{2,1,0:T(8,128)} %bitcast.15, s32[]{:T(128)S(6)} %select_n.13), kind=kLoop, calls=%fused_computation.6 | loop fusion | flops 12288 | bytes 81924 | tf_op jit(solution)/shard_map/add | solution.py:175
Async XLA Ops:
  0.0 36.7 %copy-start = (f32[32,128]{1,0:T(8,128)S(1)}, f32[32,128]{1,0:T(8,128)}, u32[]{:S(2)}) copy-start(f32[32,128]{1,0:T(8,128)} %param.8) | copy-start | bytes 49156
  0.0 5.0 %collective-permute-start = (f32[1,32,128]{2,1,0:T(8,128)}, f32[1,32,128]{2,1,0:T(8,128)S(1)}, u32[]{:S(2)}, u32[]{:S(2)}) collective-permute-start(f32[1,32,128]{2,1,0:T(8,128)} %bitcast.16), channel_id=1, source_target_pairs={{0,1},{1,0},{2,3},{3,2},{4,5},{5,4},{6,7},{7,6},{8,9},{9,8},{10,11... | collective-permute-start | bytes 49160 | tf_op jit(solution)/shard_map/ppermute | solution.py:162
  5.7 3.9 %collective-permute-start.1 = (f32[2,32,128]{2,1,0:T(8,128)S(1)}, f32[2,32,128]{2,1,0:T(8,128)S(1)}, u32[]{:S(2)}, u32[]{:S(2)}) collective-permute-start(f32[2,32,128]{2,1,0:T(8,128)S(1)} %pad_maximum_fusion.2), channel_id=1, source_target_pairs={{0,2},{1,3},{2,0},{3,1},{4,6},{5,7},{6,4},{7,5},{8,10},{9,11},{10,... | collective-permute-start | bytes 98312 | tf_op jit(solution)/shard_map/ppermute | solution.py:162
  10.3 26.4 %collective-permute-start.2 = (f32[4,32,128]{2,1,0:T(8,128)S(1)}, f32[4,32,128]{2,1,0:T(8,128)S(1)}, u32[]{:S(2)}, u32[]{:S(2)}) collective-permute-start(f32[4,32,128]{2,1,0:T(8,128)S(1)} %pad_maximum_fusion.1), channel_id=1, source_target_pairs={{0,4},{1,5},{2,6},{3,7},{4,0},{5,1},{6,2},{7,3},{8,12},{9,13},{10,... | collective-permute-start | bytes 196616 | tf_op jit(solution)/shard_map/ppermute | solution.py:162
  68.6 1.9 %collective-permute-start.3 = (f32[32,128]{1,0:T(8,128)S(1)}, f32[32,128]{1,0:T(8,128)S(1)}, u32[]{:S(2)}, u32[]{:S(2)}) collective-permute-start(f32[32,128]{1,0:T(8,128)S(1)} %get-tuple-element.5), channel_id=1, source_target_pairs={{0,8},{8,0},{16,24},{24,16},{1,9},{9,1},{17,25},{25,17},{2,10},{10... | collective-permute-start | bytes 49160 | tf_op jit(solution)/shard_map/ppermute | solution.py:175
  68.6 3.8 %collective-permute-start.4 = (f32[32,128]{1,0:T(8,128)S(1)}, f32[32,128]{1,0:T(8,128)S(1)}, u32[]{:S(2)}, u32[]{:S(2)}) collective-permute-start(f32[32,128]{1,0:T(8,128)S(1)} %get-tuple-element.7), channel_id=1, source_target_pairs={{0,16},{8,24},{16,0},{24,8},{1,17},{9,25},{17,1},{25,9},{2,18},{10... | collective-permute-start | bytes 49160 | tf_op jit(solution)/shard_map/ppermute | solution.py:175
  70.2 3.2 %collective-permute-start.5 = (f32[32,128]{1,0:T(8,128)S(1)}, f32[32,128]{1,0:T(8,128)S(1)}, u32[]{:S(2)}, u32[]{:S(2)}) collective-permute-start(f32[32,128]{1,0:T(8,128)S(1)} %get-tuple-element.6), channel_id=1, source_target_pairs={{0,24},{8,16},{16,8},{24,0},{1,25},{9,17},{17,9},{25,1},{2,26},{10... | collective-permute-start | bytes 49160 | tf_op jit(solution)/shard_map/ppermute | solution.py:175

commit v2 on v1

v2 whole, which is shorter than its diff:
```python
import functools

import jax
import jax.numpy as jnp
from jax import lax
from jax.experimental import pallas as pl
from jax.experimental.pallas import tpu as pltpu
from jax.sharding import PartitionSpec as P

BF = jnp.bfloat16
F32 = jnp.float32
I32 = jnp.int32
NT = (((1,), (1,)), ((), ()))
BLOCK = 16


def split(x):
    hi = x.astype(BF)
    return hi, (x - hi.astype(F32)).astype(BF)


def fold_kernel(rows,pairs_ref,tg_ref,sg_ref,v_ref,g_ref,vcat,wcat,rows_p,rows_t,rows_s):
    n_pairs=v_ref.shape[0]; na=g_ref.shape[2]//2
    main=n_pairs//128*128; rest=n_pairs-main
    exc=pairs_ref.shape[1]; ew=rows_p.shape[0]*128
    @pl.when(pl.program_id(0)==0)
    def _():
        hi,lo=split(v_ref[...])
        vcat[:,:main]=hi[:,:main]; vcat[:,main:2*main]=lo[:,:main]
        vcat[:,2*main:2*main+rest]=hi[:,main:]; vcat[:,2*main+rest:2*main+2*rest]=lo[:,main:]
    def row(ref,j,fill):
        r=ref[j:j+1,:]
        return r
    for jp in range(rows//2):
        for h in range(2):
            j=2*jp+h
            pr=pairs_ref[j:j+1,:]; tr=tg_ref[j:j+1,:]; sr=sg_ref[j:j+1,:].astype(F32)
            op=jnp.where(lax.broadcasted_iota(jnp.int32,(n_pairs,exc),0)==pr,1.0,0.0).astype(BF)
            tt=jnp.where(lax.broadcasted_iota(jnp.int32,(na,exc),0)==tr,sr,0.0).astype(BF)
            w=lax.dot_general(op,tt,NT,preferred_element_type=F32).astype(BF)
            c=slice(h*na,(h+1)*na)
            s=jp%2
            wcat[s,0:main,c]=w[:main]; wcat[s,main:2*main,c]=w[:main]
            wcat[s,2*main:2*main+rest,c]=w[main:]; wcat[s,2*main+rest:2*main+2*rest,c]=w[main:]
        g=jnp.dot(vcat[...],wcat[jp%2],preferred_element_type=F32)
        for h in range(2):
            j=2*jp+h
            hi,lo=split(g[:,h*na:(h+1)*na])
            g_ref[j,:n_pairs,:na]=hi; g_ref[j,:n_pairs,na:]=lo
            g_ref[j,n_pairs:,:]=jnp.zeros((g_ref.shape[1]-n_pairs,2*na),BF)
def fold(pairs,tg,sg,v,total_rows):
    rows_here,exc=pairs.shape; n_pairs=v.shape[0]; w=(n_pairs+127)//128*128
    rows=8; ew=(exc+127)//128
    main=n_pairs//128*128; rest=n_pairs-main
    kc=2*n_pairs
    tab=pl.BlockSpec((rows,exc),lambda i:(i,0))
    return pl.pallas_call(functools.partial(fold_kernel,rows),
        out_shape=jax.ShapeDtypeStruct((rows_here,w,2*total_rows),BF),
        grid=(rows_here//rows,),
        in_specs=[tab,tab,tab,pl.BlockSpec((n_pairs,n_pairs),lambda i:(0,0))],
        out_specs=pl.BlockSpec((rows,w,2*total_rows),lambda i:(i,0,0)),
        scratch_shapes=[pltpu.VMEM((n_pairs,kc),BF),pltpu.VMEM((2,kc,2*total_rows),BF),
           pltpu.VMEM((ew,rows_here,128),jnp.int32),pltpu.VMEM((ew,rows_here,128),jnp.int32),pltpu.VMEM((ew,rows_here,128),F32)],
    )(pairs,tg,sg,v)
def gath(x,idx): return jnp.take_along_axis(x,idx,axis=1,mode="promise_in_bounds")
def tree(parts,masks):
    lvl=0
    while len(parts)>1:
        parts=[jnp.where(masks[lvl],parts[2*i+1],parts[2*i]) for i in range(len(parts)//2)]; lvl+=1
    return parts[0]
def sig_kernel(parts,place,c_ref,tg_ref,sg_ref,pr_ref,g_hbm,*refs):
    outs=refs[:parts]
    tgs,sgs,prs,lift,perm,turned,gv,accr,sem=refs[parts:]
    nk,na,lanes=c_ref.shape
    exc,nb=tg_ref.shape
    ew=tgs.shape[1]; chunks=lift.shape[0]; ni=g_hbm.shape[1]//2
    cp=pltpu.make_async_copy(g_hbm,gv,sem); cp.start()
    def flip(ref): return jnp.concatenate([ref[...],jnp.zeros((ew-exc,nb),ref.dtype)],0).T
    tgs[...]=flip(tg_ref)^(place[0]*lanes); sgs[...]=flip(sg_ref).astype(F32); prs[...]=flip(pr_ref)
    bits=nk.bit_length()-1
    seg=nb//8; blk=8*(seg+1)+1
    wide=2*128; nc=(chunks*128+wide-1)//wide
    def body(g,_):
        b0=pl.multiple_of(g*BLOCK,BLOCK)
        tg8=tgs[pl.ds(b0,BLOCK),:]; sg8=sgs[pl.ds(b0,BLOCK),:]; pr8=prs[pl.ds(b0,BLOCK),:]
        for j in range(BLOCK):
            cols=[]
            for ec in range(ew//128):
                t=jnp.broadcast_to(tg8[j:j+1,ec*128:(ec+1)*128],(8,128))
                s=jnp.broadcast_to(sg8[j:j+1,ec*128:(ec+1)*128],(8,128))
                lane=t&127; ch=t>>7
                ms=[(ch&(1<<i))!=0 for i in range(bits)]
                cols.append(jnp.concatenate([tree([gath(c_ref[k,ag*8:(ag+1)*8,:],lane) for k in range(nk)],ms)*s for ag in range(na//8)],0))
            x=jnp.concatenate(cols,1)
            hi,lo=split(x)
            x=jnp.concatenate([hi,lo],0)
            p=pr8[j:j+1,:]
            pl_=p&(wide-1); pc=p>>8
            xm=[]
            for c in range(nc):
                m=jnp.where(pc==c,1.0,0.0).astype(BF)
                xm.append(x*m)
            xm=jnp.concatenate(xm,0)
            o=jnp.where(lax.broadcasted_iota(I32,(wide,ew),0).astype(BF)==pl_.astype(BF),jnp.bfloat16(1),jnp.bfloat16(0))
            r=lax.dot_general(xm,o,NT,preferred_element_type=F32)
            bb=b0+j
            row=bb+lax.div(bb,seg)
            for q in range(chunks):
                c,w=divmod(q,2); cs=slice(w*128,(w+1)*128)
                for r0 in range(0,na,8):
                    t0=c*2*na+r0
                    lift.at[q][pl.ds(row+r0*blk,8,stride=blk),:]=r[t0:t0+8,cs]+r[t0+na:t0+na+8,cs]
        return 0
    lax.fori_loop(0,nb//BLOCK,body,0)
    cp.wait()
    per=4
    def mm(ap):
        parts=[]
        for jj in range(per):
            a=per*ap+jj
            parts+=[jnp.concatenate([lift.at[q][pl.ds(a*blk+rr,8,stride=seg+1),:] for rr in range(seg)],0) for q in range(chunks)]
        hi,lo=split(jnp.concatenate(parts,1))
        kw=per*chunks*128
        return jnp.dot(jnp.concatenate([hi,lo],0),gv[pl.ds(pl.multiple_of(ap*kw,kw),kw),:],preferred_element_type=F32)
    accr[...]=mm(0)
    def st(ap,_):
        accr[...]+=mm(ap); return 0
    lax.fori_loop(1,na//per,st,0)
    acc=accr[...]
    tot=(acc[:nb,:ni]+acc[nb:,:ni])+(acc[:nb,ni:]+acc[nb:,ni:])
    for i0 in range(0,ni,128):
        for rr in range(seg):
            perm.at[i0//128][pl.ds(rr,8,stride=seg),:]=tot[rr*8:rr*8+8,i0:i0+128]
        turned[i0:i0+128,:]=perm[i0//128,:nb].T
    rows=outs[0].shape[0]
    for k in range(parts):
        outs[k][...]=turned[pl.ds(pl.multiple_of((place[1]^k)*rows,rows),rows),:]
def sig(place,c,tg,sg,pr,g,parts):
    nk,na,lanes=c.shape; exc,nb=tg.shape; chunks=g.shape[0]//na//128; ni=g.shape[1]//2
    ew=(exc+127)//128*128
    vm=pl.BlockSpec(memory_space=pltpu.VMEM)
    return pl.pallas_call(functools.partial(sig_kernel,parts),
       out_shape=[jax.ShapeDtypeStruct((ni//parts,nb),F32)]*parts,
       in_specs=[pl.BlockSpec(memory_space=pltpu.SMEM)]+[vm]*4+[pl.BlockSpec(memory_space=pl.ANY)],out_specs=[vm]*parts,
       scratch_shapes=[pltpu.VMEM((nb,ew),I32),pltpu.VMEM((nb,ew),F32),pltpu.VMEM((nb,ew),I32),
          pltpu.VMEM((chunks,(na+1)*(8*(nb//8+1)+1),128),F32),pltpu.VMEM((ni//128,nb+nb//8,128),F32),pltpu.VMEM((ni,nb),F32),
          pltpu.VMEM(g.shape,BF),pltpu.VMEM((2*nb,2*ni),F32),pltpu.SemaphoreType.DMA(())])(place,c,tg,sg,pr,g)


def local(
    coeff, integrals, beta_pairs, beta_targets, beta_signs, alpha_pairs, alpha_targets, alpha_signs
):
    n_beta = lax.axis_size("beta")
    n_alpha = lax.axis_size("alpha")
    rows, cols = coeff.shape
    table = coeff[None]
    step = 1
    while step < n_beta:
        other = lax.ppermute(table, "beta", [(i, i ^ step) for i in range(n_beta)])
        table = jnp.concatenate([table, other], 0)
        step *= 2
    place = jnp.stack([lax.axis_index("beta"), lax.axis_index("alpha")]).astype(I32)
    g = fold(alpha_pairs, alpha_targets, alpha_signs, integrals, rows * n_alpha)
    g = g.reshape(-1, g.shape[2])
    parts = sig(place, table, beta_targets.T, beta_signs.T, beta_pairs.T, g, n_alpha)
    total = parts[0]
    for k in range(1, n_alpha):
        total = total + lax.ppermute(parts[k], "alpha", [(i, i ^ k) for i in range(n_alpha)])
    return total


def solution(mesh):
    placed = (
        P("alpha", "beta"),
        P(),
        P("beta", None),
        P("beta", None),
        P("beta", None),
        P("alpha", None),
        P("alpha", None),
        P("alpha", None),
    )
    return jax.shard_map(
        local, mesh=mesh, in_specs=placed, out_specs=P("alpha", "beta"), check_vma=False
    )
```

time: 75.4 us -> 52.1 us (0.69)
  Pallas kernels: 49.9 us -> 31.1 us
  local copies, waits for them, and re-layouts: 5.05 us -> 0.01 us
  waiting for transfers between devices: 5.75 us -> 7.56 us
    pallas_call x2 -> x1, Pallas kernels: 36.4 us -> 17.6 us  [sig(): pl.pallas_call(functools.partial(sig_kernel, parts), out_shape=[jax.Shape...]
    unnamed x5 -> x2, local copies, waits for them, and re-layouts: 4.28 us -> 0.01 us
    ppermute x3, waiting for transfers between devices: 2.89 us -> 4.22 us  [local(): other = lax.ppermute(table, 'beta', [(i, i ^ step) for i in range(n_beta)])]
    squeeze x1 -> x0, local copies, waits for them, and re-layouts: 0.77 us -> none  [local(): block = lax.dynamic_index_in_dim(parts, mine ^ k, 0, False)]
  transfers between devices with their start and end apart: 6 -> 6, of which waited for: 4 -> 4; matrix products, arithmetic and copies ran while one was open for 7% -> 1% of each run, Pallas kernels for 26% -> 26%
where the time goes in v2:
time: 52.1 us; the launch traced here: 51.7 us
  Pallas kernels  31.1 us (60%)
  starting transfers between devices  9.64 us (19%)
  waiting for transfers between devices  7.56 us (15%)
  other arithmetic  3.35 us (6%)
    pallas_call x1, Pallas kernels, sig(): pl.pallas_call(functools.partial(sig_kernel, parts), out_shape=[jax.Shape...  17.6 us
    pallas_call x1, Pallas kernels, fold(): pl.pallas_call(functools.partial(fold_kernel, rows), out_shape=jax.ShapeD...  13.5 us
    ppermute x3, starting transfers between devices, local(): other = lax.ppermute(table, 'beta', [(i, i ^ step) for i in range(n_beta)])  7.63 us
    ppermute x3, waiting for transfers between devices, local(): other = lax.ppermute(table, 'beta', [(i, i ^ step) for i in range(n_beta)])  4.22 us
    ppermute x3, waiting for transfers between devices, local(): lax.ppermute(parts[k], 'alpha', [(i, i ^ k) for i in range(n_alpha)])  3.33 us
    ppermute x3, starting transfers between devices, local(): lax.ppermute(parts[k], 'alpha', [(i, i ^ k) for i in range(n_alpha)])  2.01 us
    concatenate x3, other arithmetic, local(): table = jnp.concatenate([table, other], 0)  1.39 us
    add x1, other arithmetic, local(): total + lax.ppermute(parts[k], 'alpha', [(i, i ^ k) for i in range(n_alph...  1.33 us
  transfers between devices with their start and end apart: 6, of which 4 were waited for; matrix products, arithmetic and copies ran while one was open for 1% of the time, Pallas kernels for 26%

profile of v2, /device:TPU:0, one launch (start us, length us, event | category | flops | bytes accessed | tf_op | source)
XLA Modules:
  0.0 51.7 jit_solution(10619175141371960886)
XLA Ops:
  0.0 0.0 copy-start
  0.0 3.0 %collective-permute-start = (f32[1,32,128]{2,1,0:T(8,128)}, f32[1,32,128]{2,1,0:T(8,128)S(1)}, u32[]{:S(2)}, u32[]{:S(2)}) collective-permute-start(f32[1,32,128]{2,1,0:T(8,128)} %bitcast.8), channel_id=1, source_target_pairs={{0,1},{1,0},{2,3},{3,2},{4,5},{5,4},{6,7},{7,6},{8,9},{9,8},{10,11... | collective-permute-start | bytes 49160 | tf_op jit(solution)/shard_map/ppermute | solution.py:159
  3.0 2.0 %collective-permute-done = f32[1,32,128]{2,1,0:T(8,128)S(1)} collective-permute-done((f32[1,32,128]{2,1,0:T(8,128)}, f32[1,32,128]{2,1,0:T(8,128)S(1)}, u32[]{:S(2)}, u32[]{:S(2)}) %collective-permute-start) | collective-permute-done | bytes 16416 | tf_op jit(solution)/shard_map/ppermute | solution.py:159
  5.0 0.7 %pad_maximum_fusion.2 = f32[2,32,128]{2,1,0:T(8,128)S(1)} fusion(f32[1,32,128]{2,1,0:T(8,128)S(1)} %collective-permute-done, f32[1,32,128]{2,1,0:T(8,128)} %bitcast.9), kind=kLoop, calls=%fused_computation.2 | loop fusion | flops 8192 | bytes 65536 | tf_op jit(solution)/shard_map/concatenate | solution.py:160
  5.7 2.0 %collective-permute-start.1 = (f32[2,32,128]{2,1,0:T(8,128)S(1)}, f32[2,32,128]{2,1,0:T(8,128)S(1)}, u32[]{:S(2)}, u32[]{:S(2)}) collective-permute-start(f32[2,32,128]{2,1,0:T(8,128)S(1)} %pad_maximum_fusion.2), channel_id=1, source_target_pairs={{0,2},{1,3},{2,0},{3,1},{4,6},{5,7},{6,4},{7,5},{8,10},{9,11},{10,... | collective-permute-start | bytes 98312 | tf_op jit(solution)/shard_map/ppermute | solution.py:159
  7.7 13.5 %shard_map.82 = bf16[32,640,256]{2,1,0:T(8,128)(2,1)} custom-call(s32[32,230]{1,0:T(8,128)} %pairs_ref.1, s32[32,230]{1,0:T(8,128)} %tg_ref.1, s32[32,230]{1,0:T(8,128)} %sg_ref.1, f32[528,528]{1,0:T(8,128)} %v_ref.1), custom_call_target="tpu_custom_call" | custom-call | tf_op jit(solution)/shard_map/pallas_call | solution.py:57
  21.2 0.0 collective-permute-done.1
  21.2 0.0 copy-done
  21.3 2.6 %collective-permute-start.2 = (f32[4,32,128]{2,1,0:T(8,128)S(1)}, f32[4,32,128]{2,1,0:T(8,128)S(1)}, u32[]{:S(2)}, u32[]{:S(2)}) collective-permute-start(f32[4,32,128]{2,1,0:T(8,128)S(1)} %pad_maximum_fusion.1), channel_id=1, source_target_pairs={{0,4},{1,5},{2,6},{3,7},{4,0},{5,1},{6,2},{7,3},{8,12},{9,13},{10,... | collective-permute-start | bytes 196616 | tf_op jit(solution)/shard_map/ppermute | solution.py:159
  23.9 0.6 %pad_add_fusion.place = s32[2]{0:T(128)} fusion(s32[1]{0:T(128)} %bitcast.1, s32[1]{0:T(128)} %bitcast), kind=kLoop, calls=%fused_computation.4 | loop fusion | flops 2 | bytes 16 | tf_op jit(solution)/shard_map/stack | solution.py:162
  24.5 2.2 %collective-permute-done.2 = f32[4,32,128]{2,1,0:T(8,128)S(1)} collective-permute-done((f32[4,32,128]{2,1,0:T(8,128)S(1)}, f32[4,32,128]{2,1,0:T(8,128)S(1)}, u32[]{:S(2)}, u32[]{:S(2)}) %collective-permute-start.2) | collective-permute-done | bytes 65568 | tf_op jit(solution)/shard_map/ppermute | solution.py:159
  26.7 0.7 %pad_maximum_fusion.c_ref = f32[8,32,128]{2,1,0:T(8,128)} fusion(f32[4,32,128]{2,1,0:T(8,128)S(1)} %collective-permute-done.2, f32[2,32,128]{2,1,0:T(8,128)S(1)} %collective-permute-done.1, f32[1,32,128]{2,1,0:T(8,128)S(1)} %collective-permute-done, f32[1,32,128]{2,1,0:T(8,128)S(1)} %bitcast.11), kind=kLoop, calls=%fused_computation | loop fusion | flops 98304 | bytes 262144 | tf_op jit(solution)/shard_map/concatenate | solution.py:160
  27.4 17.6 %shard_map.83 = (f32[32,128]{1,0:T(8,128)}, f32[32,128]{1,0:T(8,128)}, f32[32,128]{1,0:T(8,128)}, f32[32,128]{1,0:T(8,128)}) custom-call(s32[2]{0:T(128)} %pad_add_fusion.place, f32[8,32,128]{2,1,0:T(8,128)} %pad_maximum_fusion.c_ref, s32[230,128]{1,0:T(8,128)} %bitcast.12, s32[230,128]{1,0:T(8,128)} %bitcast.13, s32[230,128]{1,0:T(8,128)} %bitcast.14, ...), custom_call_target="tpu_custom_call" | custom-call | tf_op jit(solution)/shard_map/pallas_call | solution.py:142
  45.0 0.1 collective-permute-start.3
  45.1 1.9 %collective-permute-start.4 = (f32[32,128]{1,0:T(8,128)}, f32[32,128]{1,0:T(8,128)S(1)}, u32[]{:S(2)}, u32[]{:S(2)}) collective-permute-start(f32[32,128]{1,0:T(8,128)} %get-tuple-element.11), channel_id=1, source_target_pairs={{0,16},{8,24},{16,0},{24,8},{1,17},{9,25},{17,1},{25,9},{2,18},{10... | collective-permute-start | bytes 49160 | tf_op jit(solution)/shard_map/ppermute | solution.py:168
  47.0 0.0 collective-permute-start.5
  47.0 0.0 collective-permute-done.3
  47.0 2.1 %collective-permute-done.4 = f32[32,128]{1,0:T(8,128)S(1)} collective-permute-done((f32[32,128]{1,0:T(8,128)}, f32[32,128]{1,0:T(8,128)S(1)}, u32[]{:S(2)}, u32[]{:S(2)}) %collective-permute-start.4) | collective-permute-done | bytes 16416 | tf_op jit(solution)/shard_map/ppermute | solution.py:168
  49.1 1.3 %collective-permute-done.5 = f32[32,128]{1,0:T(8,128)S(1)} collective-permute-done((f32[32,128]{1,0:T(8,128)}, f32[32,128]{1,0:T(8,128)S(1)}, u32[]{:S(2)}, u32[]{:S(2)}) %collective-permute-start.5) | collective-permute-done | bytes 16416 | tf_op jit(solution)/shard_map/ppermute | solution.py:168
  50.4 1.3 %add_add_fusion = f32[32,128]{1,0:T(8,128)} fusion(f32[32,128]{1,0:T(8,128)S(1)} %collective-permute-done.5, f32[32,128]{1,0:T(8,128)S(1)} %collective-permute-done.4, f32[32,128]{1,0:T(8,128)} %get-tuple-element.9, f32[32,128]{1,0:T(8,128)S(1)} %collective-permute-done.3), kind=kLoop, calls=%fused_computation.3 | loop fusion | flops 12288 | bytes 81920 | tf_op jit(solution)/shard_map/add | solution.py:168
  (1 shorter events, 0.0 us)
Async XLA Ops:
  0.0 21.2 %copy-start = (f32[32,128]{1,0:T(8,128)S(1)}, f32[32,128]{1,0:T(8,128)}, u32[]{:S(2)}) copy-start(f32[32,128]{1,0:T(8,128)} %param.8) | copy-start | bytes 49156
  0.0 5.0 %collective-permute-start = (f32[1,32,128]{2,1,0:T(8,128)}, f32[1,32,128]{2,1,0:T(8,128)S(1)}, u32[]{:S(2)}, u32[]{:S(2)}) collective-permute-start(f32[1,32,128]{2,1,0:T(8,128)} %bitcast.8), channel_id=1, source_target_pairs={{0,1},{1,0},{2,3},{3,2},{4,5},{5,4},{6,7},{7,6},{8,9},{9,8},{10,11... | collective-permute-start | bytes 49160 | tf_op jit(solution)/shard_map/ppermute | solution.py:159
  5.7 15.5 %collective-permute-start.1 = (f32[2,32,128]{2,1,0:T(8,128)S(1)}, f32[2,32,128]{2,1,0:T(8,128)S(1)}, u32[]{:S(2)}, u32[]{:S(2)}) collective-permute-start(f32[2,32,128]{2,1,0:T(8,128)S(1)} %pad_maximum_fusion.2), channel_id=1, source_target_pairs={{0,2},{1,3},{2,0},{3,1},{4,6},{5,7},{6,4},{7,5},{8,10},{9,11},{10,... | collective-permute-start | bytes 98312 | tf_op jit(solution)/shard_map/ppermute | solution.py:159
  21.3 5.5 %collective-permute-start.2 = (f32[4,32,128]{2,1,0:T(8,128)S(1)}, f32[4,32,128]{2,1,0:T(8,128)S(1)}, u32[]{:S(2)}, u32[]{:S(2)}) collective-permute-start(f32[4,32,128]{2,1,0:T(8,128)S(1)} %pad_maximum_fusion.1), channel_id=1, source_target_pairs={{0,4},{1,5},{2,6},{3,7},{4,0},{5,1},{6,2},{7,3},{8,12},{9,13},{10,... | collective-permute-start | bytes 196616 | tf_op jit(solution)/shard_map/ppermute | solution.py:159
  45.0 2.0 %collective-permute-start.3 = (f32[32,128]{1,0:T(8,128)}, f32[32,128]{1,0:T(8,128)S(1)}, u32[]{:S(2)}, u32[]{:S(2)}) collective-permute-start(f32[32,128]{1,0:T(8,128)} %get-tuple-element.10), channel_id=1, source_target_pairs={{0,8},{8,0},{16,24},{24,16},{1,9},{9,1},{17,25},{25,17},{2,10},{10... | collective-permute-start | bytes 49160 | tf_op jit(solution)/shard_map/ppermute | solution.py:168
  45.1 4.0 %collective-permute-start.4 = (f32[32,128]{1,0:T(8,128)}, f32[32,128]{1,0:T(8,128)S(1)}, u32[]{:S(2)}, u32[]{:S(2)}) collective-permute-start(f32[32,128]{1,0:T(8,128)} %get-tuple-element.11), channel_id=1, source_target_pairs={{0,16},{8,24},{16,0},{24,8},{1,17},{9,25},{17,1},{25,9},{2,18},{10... | collective-permute-start | bytes 49160 | tf_op jit(solution)/shard_map/ppermute | solution.py:168
  47.0 3.4 %collective-permute-start.5 = (f32[32,128]{1,0:T(8,128)}, f32[32,128]{1,0:T(8,128)S(1)}, u32[]{:S(2)}, u32[]{:S(2)}) collective-permute-start(f32[32,128]{1,0:T(8,128)} %get-tuple-element.12), channel_id=1, source_target_pairs={{0,24},{8,16},{16,8},{24,0},{1,25},{9,17},{17,9},{25,1},{2,26},{10... | collective-permute-start | bytes 49160 | tf_op jit(solution)/shard_map/ppermute | solution.py:168

commit v3 on v2

v3 whole, which is shorter than its diff:
```python
import functools

import jax
import jax.numpy as jnp
from jax import lax
from jax.experimental import pallas as pl
from jax.experimental.pallas import tpu as pltpu
from jax.sharding import PartitionSpec as P

BF = jnp.bfloat16
F32 = jnp.float32
I32 = jnp.int32
NT = (((1,), (1,)), ((), ()))
BLOCK = 16
PAIRED = 1


def split(x):
    hi = x.astype(BF)
    return hi, (x - hi.astype(F32)).astype(BF)


def fold_kernel(rows,pairs_ref,tg_ref,sg_ref,v_ref,g_ref,vcat,wcat):
    n_pairs=v_ref.shape[0]; na=g_ref.shape[2]//2
    main=n_pairs//128*128; rest=n_pairs-main
    exc=pairs_ref.shape[1]
    @pl.when(pl.program_id(0)==0)
    def _():
        hi,lo=split(v_ref[...])
        vcat[:,:main]=hi[:,:main]; vcat[:,main:2*main]=lo[:,:main]
        vcat[:,2*main:2*main+rest]=hi[:,main:]; vcat[:,2*main+rest:2*main+2*rest]=lo[:,main:]
    def spread(jp):
        for h in range(2):
            j=2*jp+h
            pr=pairs_ref[j:j+1,:]; tr=tg_ref[j:j+1,:].astype(BF); sr=sg_ref[j:j+1,:].astype(BF)
            ops=[]
            for q0 in range(0,n_pairs,256):
                n=min(256,n_pairs-q0)
                ops.append(jnp.where(lax.broadcasted_iota(I32,(n,exc),0).astype(BF)==(pr-q0).astype(BF),jnp.bfloat16(1),jnp.bfloat16(0)))
            op=jnp.concatenate(ops,0)
            tt=jnp.where(lax.broadcasted_iota(I32,(na,exc),0).astype(BF)==tr,sr,jnp.bfloat16(0))
            w=lax.dot_general(op,tt,NT,preferred_element_type=F32).astype(BF)
            c=slice(h*na,(h+1)*na); s=jp%2
            wcat[s,0:main,c]=w[:main]; wcat[s,main:2*main,c]=w[:main]
            wcat[s,2*main:2*main+rest,c]=w[main:]; wcat[s,2*main+rest:2*main+2*rest,c]=w[main:]
    def mix(jp):
        g=jnp.dot(vcat[...],wcat[jp%2],preferred_element_type=F32)
        for h in range(2):
            j=2*jp+h
            hi,lo=split(g[:,h*na:(h+1)*na])
            g_ref[j,:n_pairs,:na]=hi; g_ref[j,:n_pairs,na:]=lo
            g_ref[j,n_pairs:,:]=jnp.zeros((g_ref.shape[1]-n_pairs,2*na),BF)
    n=rows//2
    spread(0)
    for jp in range(n):
        if jp+1<n: spread(jp+1)
        mix(jp)
def fold(pairs,tg,sg,v,total_rows):
    rows_here,exc=pairs.shape; n_pairs=v.shape[0]; w=(n_pairs+127)//128*128
    rows=8
    kc=2*n_pairs
    tab=pl.BlockSpec((rows,exc),lambda i:(i,0))
    return pl.pallas_call(functools.partial(fold_kernel,rows),
        out_shape=jax.ShapeDtypeStruct((rows_here,w,2*total_rows),BF),
        grid=(rows_here//rows,),
        in_specs=[tab,tab,tab,pl.BlockSpec((n_pairs,n_pairs),lambda i:(0,0))],
        out_specs=pl.BlockSpec((rows,w,2*total_rows),lambda i:(i,0,0)),
        scratch_shapes=[pltpu.VMEM((n_pairs,kc),BF),pltpu.VMEM((2,kc,2*total_rows),BF)],
    )(pairs,tg,sg,v)
def gath(x,idx): return jnp.take_along_axis(x,idx,axis=1,mode="promise_in_bounds")
def tree(parts,masks,low=0,bit=None):
    bit=len(masks) if bit is None else bit
    if bit==0: return parts.get(low)
    left=tree(parts,masks,low,bit-1); right=tree(parts,masks,low+(1<<(bit-1)),bit-1)
    if left is None: return right
    return left if right is None else jnp.where(masks[bit-1],right,left)
def sig_kernel(parts,direct,place,c_ref,tg_ref,sg_ref,pr_ref,g_hbm,*refs):
    outs=refs[:parts]
    tgs,sgs,prs,cs_ref,xf,rs,lift,perm,turned,gv,accr,sem=refs[parts:]
    nk,na,lanes=c_ref.shape
    exc,nb=tg_ref.shape
    ew=tgs.shape[1]; chunks=lift.shape[0]; ni=g_hbm.shape[1]//2
    cp=pltpu.make_async_copy(g_hbm,gv,sem); cp.start()
    def flip(ref): return jnp.concatenate([ref[...],jnp.zeros((ew-exc,nb),ref.dtype)],0).T
    tgs[...]=flip(tg_ref) if direct else flip(tg_ref)^(place[0]*lanes); sgs[...]=flip(sg_ref).astype(F32); prs[...]=flip(pr_ref)
    bits=nk.bit_length()-1
    if PAIRED:
        hi,lo=split(jnp.concatenate([c_ref[k] for k in range(2*PAIRED)],1))
        cs_ref[:na]=hi; cs_ref[na:]=lo
    seg=nb//8; blk=8*(seg+1)+1
    wide=2*128; nc=(chunks*128+wide-1)//wide
    def early(g,slot):
        b0=pl.multiple_of(g*BLOCK,BLOCK)
        tg8=tgs[pl.ds(b0,BLOCK),:]; sg8=sgs[pl.ds(b0,BLOCK),:]
        for j in range(BLOCK):
            tb=tg8[j:j+1,:]; sb=sg8[j:j+1,:].astype(BF)
            o2=jnp.concatenate([jnp.where(lax.broadcasted_iota(I32,(256,ew),0).astype(BF)==(tb-256*m).astype(BF),sb,jnp.bfloat16(0)) for m in range(PAIRED)],0)
            rg=jnp.dot(cs_ref[...],o2,preferred_element_type=F32)
            rs[slot,j]=rg[:na]+rg[na:]
            yield
    def gather(g,slot):
        b0=pl.multiple_of(g*BLOCK,BLOCK)
        tg8=tgs[pl.ds(b0,BLOCK),:]; sg8=sgs[pl.ds(b0,BLOCK),:]
        for j in range(BLOCK):
            cols=[]
            for ec in range(ew//128):
                t=jnp.broadcast_to(tg8[j:j+1,ec*128:(ec+1)*128],(8,128))
                s=jnp.broadcast_to(sg8[j:j+1,ec*128:(ec+1)*128],(8,128))
                lane=t&127; ch=t>>7
                ms=[(ch&(1<<i))!=0 for i in range(bits)]
                s=jnp.where(ch<2*PAIRED,0.0,s)
                for ag in range(na//8):
                    v=tree({k:gath(c_ref[k,ag*8:(ag+1)*8,:],lane) for k in range(2*PAIRED,nk)},ms)*s
                    xf[slot,j,ag*8:ag*8+8,ec*128:(ec+1)*128]=v
            yield
    def raise_(g,slot):
        b0=pl.multiple_of(g*BLOCK,BLOCK)
        pr8=prs[pl.ds(b0,BLOCK),:]
        for j in range(BLOCK):
            p=pr8[j:j+1,:]
            pl_=p&(wide-1); pc=p>>8
            x=xf[slot,j]
            if PAIRED: x=x+rs[slot,j]
            hi,lo=split(x)
            x=jnp.concatenate([hi,lo],0)
            xm=jnp.concatenate([x*jnp.where(pc==c,1.0,0.0).astype(BF) for c in range(nc)],0)
            o=jnp.where(lax.broadcasted_iota(I32,(wide,ew),0).astype(BF)==pl_.astype(BF),jnp.bfloat16(1),jnp.bfloat16(0))
            r=lax.dot_general(xm,o,NT,preferred_element_type=F32)
            bb=b0+j
            row=bb+lax.div(bb,seg)
            for q in range(chunks):
                c,w=divmod(q,2); cw=slice(w*128,(w+1)*128)
                for r0 in range(0,na,8):
                    t0=c*2*na+r0
                    lift.at[q][pl.ds(row+r0*blk,8,stride=blk),:]=r[t0:t0+8,cw]+r[t0+na:t0+na+8,cw]
            yield
    def drive(*gens):
        for _ in range(BLOCK):
            for gen in gens: next(gen)
    groups=nb//BLOCK
    def load(g,slot): return ((early(g,slot),) if PAIRED else ())+(gather(g,slot),)
    drive(*load(0,0))
    def body(g,_):
        slot=g&1
        drive(raise_(g,slot),*load(g+1,1-slot))
        return 0
    lax.fori_loop(0,groups-1,body,0)
    drive(raise_(groups-1,(groups-1)&1))
    cp.wait()
    per=4
    def mm(ap):
        parts=[]
        for jj in range(per):
            a=per*ap+jj
            parts+=[jnp.concatenate([lift.at[q][pl.ds(a*blk+rr,8,stride=seg+1),:] for rr in range(seg)],0) for q in range(chunks)]
        hi,lo=split(jnp.concatenate(parts,1))
        kw=per*chunks*128
        return jnp.dot(jnp.concatenate([hi,lo],0),gv[pl.ds(pl.multiple_of(ap*kw,kw),kw),:],preferred_element_type=F32)
    accr[...]=mm(0)
    def st(ap,_):
        accr[...]+=mm(ap); return 0
    lax.fori_loop(1,na//per,st,0)
    acc=accr[...]
    tot=(acc[:nb,:ni]+acc[nb:,:ni])+(acc[:nb,ni:]+acc[nb:,ni:])
    for i0 in range(0,ni,128):
        for rr in range(seg):
            perm.at[i0//128][pl.ds(rr,8,stride=seg),:]=tot[rr*8:rr*8+8,i0:i0+128]
        turned[i0:i0+128,:]=perm[i0//128,:nb].T
    rows=outs[0].shape[0]
    for k in range(parts):
        outs[k][...]=turned[pl.ds(pl.multiple_of((place[1]^k)*rows,rows),rows),:]
def sig(place,c,tg,sg,pr,g,parts,direct):
    nk,na,lanes=c.shape; exc,nb=tg.shape; chunks=g.shape[0]//na//128; ni=g.shape[1]//2
    ew=(exc+127)//128*128
    vm=pl.BlockSpec(memory_space=pltpu.VMEM)
    return pl.pallas_call(functools.partial(sig_kernel,parts,direct),
       out_shape=[jax.ShapeDtypeStruct((ni//parts,nb),F32)]*parts,
       in_specs=[pl.BlockSpec(memory_space=pltpu.SMEM)]+[vm]*4+[pl.BlockSpec(memory_space=pl.ANY)],out_specs=[vm]*parts,
       scratch_shapes=[pltpu.VMEM((nb,ew),I32),pltpu.VMEM((nb,ew),F32),pltpu.VMEM((nb,ew),I32),pltpu.VMEM((2*na,256*max(PAIRED,1)),BF),pltpu.VMEM((2,BLOCK,na,ew),F32),pltpu.VMEM((2,BLOCK,na,ew),F32),
          pltpu.VMEM((chunks,(na+1)*(8*(nb//8+1)+1),128),F32),pltpu.VMEM((ni//128,nb+nb//8,128),F32),pltpu.VMEM((ni,nb),F32),pltpu.VMEM(g.shape,BF),pltpu.VMEM((2*nb,2*ni),F32),pltpu.SemaphoreType.DMA(())])(place,c,tg,sg,pr,g)


def local(
    coeff, integrals, beta_pairs, beta_targets, beta_signs, alpha_pairs, alpha_targets, alpha_signs
):
    n_beta = lax.axis_size("beta")
    n_alpha = lax.axis_size("alpha")
    rows, cols = coeff.shape
    table = jnp.broadcast_to(coeff[None], (n_beta, rows, cols))
    table = lax.all_to_all(table, "beta", 0, 0)
    place = jnp.stack([lax.axis_index("beta"), lax.axis_index("alpha")]).astype(I32)
    g = fold(alpha_pairs, alpha_targets, alpha_signs, integrals, rows * n_alpha)
    g = g.reshape(-1, g.shape[2])
    parts = sig(place, table, beta_targets.T, beta_signs.T, beta_pairs.T, g, n_alpha, True)
    total = parts[0]
    for k in range(1, n_alpha):
        total = total + lax.ppermute(parts[k], "alpha", [(i, i ^ k) for i in range(n_alpha)])
    return total


def solution(mesh):
    placed = (
        P("alpha", "beta"),
        P(),
        P("beta", None),
        P("beta", None),
        P("beta", None),
        P("alpha", None),
        P("alpha", None),
        P("alpha", None),
    )
    return jax.shard_map(
        local, mesh=mesh, in_specs=placed, out_specs=P("alpha", "beta"), check_vma=False
    )
```

time: 52.1 us -> 45.8 us (0.88)
  waiting for transfers between devices: 7.56 us -> 3.12 us
  Pallas kernels: 31.1 us -> 29 us
  local copies, waits for them, and re-layouts: 0.01 us -> 2.03 us
  other arithmetic: 3.35 us -> 1.94 us
    ppermute x3 -> x0, starting transfers between devices: 7.63 us -> none  [local(): other = lax.ppermute(table, 'beta', [(i, i ^ step) for i in range(n_beta)])]
    all_to_all x0 -> x1, starting transfers between devices: none -> 7.28 us  [local(): table = lax.all_to_all(table, 'beta', 0, 0)]
    ppermute x3 -> x0, waiting for transfers between devices: 4.22 us -> none  [local(): other = lax.ppermute(table, 'beta', [(i, i ^ step) for i in range(n_beta)])]
    concatenate x3 -> x0, other arithmetic: 1.39 us -> none  [local(): table = jnp.concatenate([table, other], 0)]
    broadcast_in_dim x0 -> x1, local copies, waits for them, and re-layouts: none -> 1.38 us  [local(): table = jnp.broadcast_to(coeff[None], (n_beta, rows, cols))]
    pallas_call x1, Pallas kernels: 13.5 us -> 12.4 us  [fold(): pl.pallas_call(functools.partial(fold_kernel, rows), out_shape=jax.ShapeD...]
    pallas_call x1, Pallas kernels: 17.6 us -> 16.5 us  [sig(): pl.pallas_call(functools.partial(sig_kernel, parts, direct), out_shape=[j...]
    unnamed x2, local copies, waits for them, and re-layouts: 0.01 us -> 0.65 us
  transfers between devices with their start and end apart: 6 -> 4, of which waited for: 4 -> 2; matrix products, arithmetic and copies ran while one was open for 1% -> 1% of each run, Pallas kernels for 26% -> 27%
where the time goes in v3:
time: 45.8 us; the launch traced here: 45.3 us
  Pallas kernels  29 us (63%)
  starting transfers between devices  9.2 us (20%)
  waiting for transfers between devices  3.12 us (7%)
  local copies, waits for them, and re-layouts  2.03 us (4%)
  other arithmetic  1.94 us (4%)
    pallas_call x1, Pallas kernels, sig(): pl.pallas_call(functools.partial(sig_kernel, parts, direct), out_shape=[j...  16.5 us
    pallas_call x1, Pallas kernels, fold(): pl.pallas_call(functools.partial(fold_kernel, rows), out_shape=jax.ShapeD...  12.4 us
    all_to_all x1, starting transfers between devices, local(): table = lax.all_to_all(table, 'beta', 0, 0)  7.28 us
    ppermute x3, waiting for transfers between devices, local(): lax.ppermute(parts[k], 'alpha', [(i, i ^ k) for i in range(n_alpha)])  3.11 us
    ppermute x3, starting transfers between devices, local(): lax.ppermute(parts[k], 'alpha', [(i, i ^ k) for i in range(n_alpha)])  1.92 us
    broadcast_in_dim x1, local copies, waits for them, and re-layouts, local(): table = jnp.broadcast_to(coeff[None], (n_beta, rows, cols))  1.38 us
    add x1, other arithmetic, local(): total + lax.ppermute(parts[k], 'alpha', [(i, i ^ k) for i in range(n_alph...  1.33 us
  transfers between devices with their start and end apart: 4, of which 2 were waited for; matrix products, arithmetic and copies ran while one was open for 1% of the time, Pallas kernels for 27%

profile of v3, /device:TPU:0, one launch (start us, length us, event | category | flops | bytes accessed | tf_op | source)
XLA Modules:
  0.0 45.3 jit_solution(8459531042587171835)
XLA Ops:
  0.0 1.4 %broadcast_in_dim.2 = f32[8,32,128]{2,1,0:T(8,128)} broadcast(f32[32,128]{1,0:T(8,128)} %param.8), dimensions={1,2} | broadcast | bytes 147456 | tf_op jit(solution)/shard_map/broadcast_in_dim | solution.py:189
  1.4 7.3 %all-to-all-start = ((f32[8,32,128]{2,1,0:T(8,128)}), f32[8,32,128]{2,1,0:T(8,128)S(1)}, u32[]{:S(2)}, u32[]{:S(2)}) async-start(f32[8,32,128]{2,1,0:T(8,128)} %broadcast_in_dim.2), calls=%async_computation | async-start | bytes 262144 | tf_op jit(solution)/shard_map/all_to_all | solution.py:190
  8.7 12.4 %shard_map.82 = bf16[32,640,256]{2,1,0:T(8,128)(2,1)} custom-call(s32[32,230]{1,0:T(8,128)} %pairs_ref.1, s32[32,230]{1,0:T(8,128)} %tg_ref.1, s32[32,230]{1,0:T(8,128)} %sg_ref.1, f32[528,528]{1,0:T(8,128)} %v_ref.1), custom_call_target="tpu_custom_call" | custom-call | tf_op jit(solution)/shard_map/pallas_call | solution.py:63
  21.1 0.6 %pad_add_fusion.place = s32[2]{0:T(128)} fusion(s32[1]{0:T(128)} %bitcast.1, s32[1]{0:T(128)} %bitcast), kind=kLoop, calls=%fused_computation.1 | loop fusion | flops 2 | bytes 16 | tf_op jit(solution)/shard_map/stack | solution.py:191
  21.7 0.0 all-to-all-done.c_ref
  21.7 0.0 copy-start
  21.7 0.7 %copy-done = f32[8,32,128]{2,1,0:T(8,128)} copy-done((f32[8,32,128]{2,1,0:T(8,128)}, f32[8,32,128]{2,1,0:T(8,128)S(1)}, u32[]{:S(2)}) %copy-start) | copy-done | bytes 131096
  22.3 16.5 %shard_map.83 = (f32[32,128]{1,0:T(8,128)}, f32[32,128]{1,0:T(8,128)}, f32[32,128]{1,0:T(8,128)}, f32[32,128]{1,0:T(8,128)}) custom-call(s32[2]{0:T(128)} %pad_add_fusion.place, f32[8,32,128]{2,1,0:T(8,128)} %copy-done, s32[230,128]{1,0:T(8,128)} %bitcast.7, s32[230,128]{1,0:T(8,128)} %bitcast.8, s32[230,128]{1,0:T(8,128)} %bitcast.9, bf16[20480,256]{1,0:T(8,128)(2,1)} %bitcast.6), custom_call_target="tpu_custom_call" | custom-call | tf_op jit(solution)/shard_map/pallas_call | solution.py:176
  38.9 0.1 collective-permute-start
  39.0 1.6 %collective-permute-start.1 = (f32[32,128]{1,0:T(8,128)}, f32[32,128]{1,0:T(8,128)S(1)}, u32[]{:S(2)}, u32[]{:S(2)}) collective-permute-start(f32[32,128]{1,0:T(8,128)} %get-tuple-element.11), channel_id=1, source_target_pairs={{0,16},{8,24},{16,0},{24,8},{1,17},{9,25},{17,1},{25,9},{2,18},{10... | collective-permute-start | bytes 49160 | tf_op jit(solution)/shard_map/ppermute | solution.py:197
  40.6 0.3 collective-permute-start.2
  40.8 0.0 collective-permute-done
  40.8 2.2 %collective-permute-done.1 = f32[32,128]{1,0:T(8,128)S(1)} collective-permute-done((f32[32,128]{1,0:T(8,128)}, f32[32,128]{1,0:T(8,128)S(1)}, u32[]{:S(2)}, u32[]{:S(2)}) %collective-permute-start.1) | collective-permute-done | bytes 16416 | tf_op jit(solution)/shard_map/ppermute | solution.py:197
  43.0 0.9 %collective-permute-done.2 = f32[32,128]{1,0:T(8,128)S(1)} collective-permute-done((f32[32,128]{1,0:T(8,128)}, f32[32,128]{1,0:T(8,128)S(1)}, u32[]{:S(2)}, u32[]{:S(2)}) %collective-permute-start.2) | collective-permute-done | bytes 16416 | tf_op jit(solution)/shard_map/ppermute | solution.py:197
  43.9 1.3 %add_add_fusion = f32[32,128]{1,0:T(8,128)} fusion(f32[32,128]{1,0:T(8,128)S(1)} %collective-permute-done.2, f32[32,128]{1,0:T(8,128)S(1)} %collective-permute-done.1, f32[32,128]{1,0:T(8,128)} %get-tuple-element.9, f32[32,128]{1,0:T(8,128)S(1)} %collective-permute-done), kind=kLoop, calls=%fused_computation | loop fusion | flops 12288 | bytes 81920 | tf_op jit(solution)/shard_map/add | solution.py:197
Async XLA Ops:
  1.4 20.3 %all-to-all-start = ((f32[8,32,128]{2,1,0:T(8,128)}), f32[8,32,128]{2,1,0:T(8,128)S(1)}, u32[]{:S(2)}, u32[]{:S(2)}) async-start(f32[8,32,128]{2,1,0:T(8,128)} %broadcast_in_dim.2), calls=%async_computation | async-start | bytes 262144 | tf_op jit(solution)/shard_map/all_to_all | solution.py:190
  21.7 0.7 %copy-start = (f32[8,32,128]{2,1,0:T(8,128)}, f32[8,32,128]{2,1,0:T(8,128)S(1)}, u32[]{:S(2)}) copy-start(f32[8,32,128]{2,1,0:T(8,128)S(1)} %all-to-all-done.c_ref) | copy-start | bytes 393220
  38.9 1.9 %collective-permute-start = (f32[32,128]{1,0:T(8,128)}, f32[32,128]{1,0:T(8,128)S(1)}, u32[]{:S(2)}, u32[]{:S(2)}) collective-permute-start(f32[32,128]{1,0:T(8,128)} %get-tuple-element.10), channel_id=1, source_target_pairs={{0,8},{8,0},{16,24},{24,16},{1,9},{9,1},{17,25},{25,17},{2,10},{10... | collective-permute-start | bytes 49160 | tf_op jit(solution)/shard_map/ppermute | solution.py:197
  39.0 4.0 %collective-permute-start.1 = (f32[32,128]{1,0:T(8,128)}, f32[32,128]{1,0:T(8,128)S(1)}, u32[]{:S(2)}, u32[]{:S(2)}) collective-permute-start(f32[32,128]{1,0:T(8,128)} %get-tuple-element.11), channel_id=1, source_target_pairs={{0,16},{8,24},{16,0},{24,8},{1,17},{9,25},{17,1},{25,9},{2,18},{10... | collective-permute-start | bytes 49160 | tf_op jit(solution)/shard_map/ppermute | solution.py:197
  40.6 3.4 %collective-permute-start.2 = (f32[32,128]{1,0:T(8,128)}, f32[32,128]{1,0:T(8,128)S(1)}, u32[]{:S(2)}, u32[]{:S(2)}) collective-permute-start(f32[32,128]{1,0:T(8,128)} %get-tuple-element.12), channel_id=1, source_target_pairs={{0,24},{8,16},{16,8},{24,0},{1,25},{9,17},{17,9},{25,1},{2,26},{10... | collective-permute-start | bytes 49160 | tf_op jit(solution)/shard_map/ppermute | solution.py:197

commit v4 on v3

v4 whole, which is shorter than its diff:
```python
import functools

import jax
import jax.numpy as jnp
from jax import lax
from jax.experimental import pallas as pl
from jax.experimental.pallas import tpu as pltpu
from jax.sharding import PartitionSpec as P

BF = jnp.bfloat16
F32 = jnp.float32
I32 = jnp.int32
NT = (((1,), (1,)), ((), ()))
BLOCK = 16
PAIRED = 1
GRANT_P = 30 * 2**20
GRANT_A = 30 * 2**20
GRANT_B = 30 * 2**20


def split(x):
    hi = x.astype(BF)
    return hi, (x - hi.astype(F32)).astype(BF)


def prepare_kernel(v_hbm, pairs_hbm, tg_hbm, sg_hbm, vcat, tabs, v_v, sems):
    pieces = ((v_hbm, v_v), (pairs_hbm, tabs.at[0]), (tg_hbm, tabs.at[1]), (sg_hbm, tabs.at[2]))
    copies = [pltpu.make_async_copy(src, dst, sems.at[k]) for k, (src, dst) in enumerate(pieces)]
    for copy in copies:
        copy.start()
    for copy in copies:
        copy.wait()
    n_pairs = v_v.shape[0]
    main = n_pairs // 128 * 128
    rest = n_pairs - main
    hi, lo = split(v_v[...])
    vcat[:, :main] = hi[:, :main]
    vcat[:, main : 2 * main] = lo[:, :main]
    if rest:
        vcat[:, 2 * main : 2 * main + rest] = hi[:, main:]
        vcat[:, 2 * main + rest : 2 * main + 2 * rest] = lo[:, main:]


def prepare(*args):
    v, pairs = args[:2]
    vm = pl.BlockSpec(memory_space=pltpu.VMEM)
    hbm = pl.BlockSpec(memory_space=pltpu.MemorySpace.HBM)
    args = [pltpu.with_memory_space_constraint(x, pltpu.MemorySpace.HBM) for x in args]
    return pl.pallas_call(
        prepare_kernel,
        out_shape=[
            jax.ShapeDtypeStruct((v.shape[0], 2 * v.shape[0]), BF),
            jax.ShapeDtypeStruct((3,) + pairs.shape, I32),
        ],
        in_specs=[hbm] * 4,
        out_specs=[vm] * 2,
        scratch_shapes=[pltpu.VMEM(v.shape, F32), pltpu.SemaphoreType.DMA((4,))],
        compiler_params=pltpu.CompilerParams(vmem_limit_bytes=GRANT_P),
        cost_estimate=pl.CostEstimate(flops=10**6, bytes_accessed=3 * 10**6, transcendentals=0),
    )(*args)


def fold_kernel(vcat, tabs, g_ref, wcat):
    n_pairs = vcat.shape[0]
    na = g_ref.shape[1] // 2
    _, rows, _ = tabs.shape
    width = g_ref.shape[0] // rows
    main = n_pairs // 128 * 128
    rest = n_pairs - main

    def group(g, _):
        a0 = pl.multiple_of(g * 8, 8)
        pairs8, tg8, sg8 = (tabs[k, pl.ds(a0, 8), :] for k in range(3))

        def spread(jp):
            for h in range(2):
                j = 2 * jp + h
                op = one_hot(pairs8[j : j + 1, :], n_pairs, None)
                tt = one_hot(tg8[j : j + 1, :], na, sg8[j : j + 1, :].astype(BF))
                w = lax.dot_general(op, tt, NT, preferred_element_type=F32).astype(BF)
                c = slice(h * na, (h + 1) * na)
                s = jp % 2
                wcat[s, 0:main, c] = w[:main]
                wcat[s, main : 2 * main, c] = w[:main]
                if rest:
                    wcat[s, 2 * main : 2 * main + rest, c] = w[main:]
                    wcat[s, 2 * main + rest : 2 * main + 2 * rest, c] = w[main:]

        def mix(jp):
            g2 = jnp.dot(vcat[...], wcat[jp % 2], preferred_element_type=F32)
            for h in range(2):
                a = a0 + 2 * jp + h
                hi, lo = split(g2[:, h * na : (h + 1) * na])
                at = pl.multiple_of(a * width, 128)
                g_ref[pl.ds(at, n_pairs), :na] = hi
                g_ref[pl.ds(at, n_pairs), na:] = lo
                g_ref[pl.ds(pl.multiple_of(at + n_pairs, 16), width - n_pairs), :] = jnp.zeros((width - n_pairs, 2 * na), BF)

        spread(0)
        for jp in range(4):
            if jp < 3:
                spread(jp + 1)
            mix(jp)
        return 0

    lax.fori_loop(0, rows // 8, group, 0)


def one_hot(row, size, value):
    one = jnp.bfloat16(1) if value is None else value
    parts = []
    for start in range(0, size, 256):
        n = min(256, size - start)
        ids = lax.broadcasted_iota(I32, (n, row.shape[1]), 0).astype(BF)
        parts.append(jnp.where(ids == (row - start).astype(BF), one, jnp.bfloat16(0)))
    return jnp.concatenate(parts, 0)


def fold(vcat, tabs, total_rows):
    n_pairs = vcat.shape[0]
    width = (n_pairs + 127) // 128 * 128
    vm = pl.BlockSpec(memory_space=pltpu.VMEM)
    return pl.pallas_call(
        fold_kernel,
        out_shape=jax.ShapeDtypeStruct((tabs.shape[1] * width, 2 * total_rows), BF),
        in_specs=[vm] * 2,
        out_specs=vm,
        scratch_shapes=[pltpu.VMEM((2, 2 * n_pairs, 2 * total_rows), BF)],
        compiler_params=pltpu.CompilerParams(vmem_limit_bytes=GRANT_A),
        cost_estimate=pl.CostEstimate(flops=10 * 10**9, bytes_accessed=12 * 10**6, transcendentals=0),
    )(vcat, tabs)


def gath(x,idx): return jnp.take_along_axis(x,idx,axis=1,mode="promise_in_bounds")


def tree(parts,masks,low=0,bit=None):
    bit=len(masks) if bit is None else bit
    if bit==0: return parts.get(low)
    left=tree(parts,masks,low,bit-1); right=tree(parts,masks,low+(1<<(bit-1)),bit-1)
    if left is None: return right
    return left if right is None else jnp.where(masks[bit-1],right,left)


def sig_kernel(parts,count,*args):
    c_refs=args[:count]
    tg_ref,sg_ref,pr_ref,gv,*refs=args[count:]
    outs=refs[:parts]
    tgs,sgs,prs,cs_ref,xf,rs,lift,perm,turned,accr=refs[parts:]
    per_ref,na,lanes=c_refs[0].shape; nk=count*per_ref
    def chunk(k): return c_refs[k//per_ref].at[k%per_ref]
    exc,nb=tg_ref.shape
    ew=tgs.shape[1]; chunks=lift.shape[0]; ni=gv.shape[1]//2
    def flip(ref): return jnp.concatenate([ref[...],jnp.zeros((ew-exc,nb),ref.dtype)],0).T
    tgs[...]=flip(tg_ref)^(lax.axis_index("beta")*lanes); sgs[...]=flip(sg_ref).astype(F32); prs[...]=flip(pr_ref)
    bits=nk.bit_length()-1
    if PAIRED:
        hi,lo=split(jnp.concatenate([chunk(k)[...] for k in range(2*PAIRED)],1))
        cs_ref[:na]=hi; cs_ref[na:]=lo
    seg=nb//8; blk=8*(seg+1)+1
    wide=2*128; nc=(chunks*128+wide-1)//wide
    def early(g,slot):
        b0=pl.multiple_of(g*BLOCK,BLOCK)
        tg8=tgs[pl.ds(b0,BLOCK),:]; sg8=sgs[pl.ds(b0,BLOCK),:]
        for j in range(BLOCK):
            tb=tg8[j:j+1,:]; sb=sg8[j:j+1,:].astype(BF)
            o2=jnp.concatenate([jnp.where(lax.broadcasted_iota(I32,(256,ew),0).astype(BF)==(tb-256*m).astype(BF),sb,jnp.bfloat16(0)) for m in range(PAIRED)],0)
            rg=jnp.dot(cs_ref[...],o2,preferred_element_type=F32)
            rs[slot,j]=rg[:na]+rg[na:]
            yield
    def gather(g,slot):
        b0=pl.multiple_of(g*BLOCK,BLOCK)
        tg8=tgs[pl.ds(b0,BLOCK),:]; sg8=sgs[pl.ds(b0,BLOCK),:]
        for j in range(BLOCK):
            for ec in range(ew//128):
                t=jnp.broadcast_to(tg8[j:j+1,ec*128:(ec+1)*128],(8,128))
                s=jnp.broadcast_to(sg8[j:j+1,ec*128:(ec+1)*128],(8,128))
                lane=t&127; ch=t>>7
                ms=[(ch&(1<<i))!=0 for i in range(bits)]
                s=jnp.where(ch<2*PAIRED,0.0,s)
                for ag in range(na//8):
                    v=tree({k:gath(chunk(k)[ag*8:(ag+1)*8,:],lane) for k in range(2*PAIRED,nk)},ms)*s
                    xf[slot,j,ag*8:ag*8+8,ec*128:(ec+1)*128]=v
            yield
    def raise_(g,slot):
        b0=pl.multiple_of(g*BLOCK,BLOCK)
        pr8=prs[pl.ds(b0,BLOCK),:]
        for j in range(BLOCK):
            p=pr8[j:j+1,:]
            pl_=p&(wide-1); pc=p>>8
            x=xf[slot,j]
            if PAIRED: x=x+rs[slot,j]
            hi,lo=split(x)
            x=jnp.concatenate([hi,lo],0)
            xm=jnp.concatenate([x*jnp.where(pc==c,1.0,0.0).astype(BF) for c in range(nc)],0)
            o=jnp.where(lax.broadcasted_iota(I32,(wide,ew),0).astype(BF)==pl_.astype(BF),jnp.bfloat16(1),jnp.bfloat16(0))
            r=lax.dot_general(xm,o,NT,preferred_element_type=F32)
            bb=b0+j
            row=bb+lax.div(bb,seg)
            for q in range(chunks):
                c,w=divmod(q,2); cw=slice(w*128,(w+1)*128)
                for r0 in range(0,na,8):
                    t0=c*2*na+r0
                    lift.at[q][pl.ds(row+r0*blk,8,stride=blk),:]=r[t0:t0+8,cw]+r[t0+na:t0+na+8,cw]
            yield
    def drive(*gens):
        for _ in range(BLOCK):
            for gen in gens: next(gen)
    groups=nb//BLOCK
    def load(g,slot): return ((early(g,slot),) if PAIRED else ())+(gather(g,slot),)
    drive(*load(0,0))
    def body(g,_):
        slot=g&1
        drive(raise_(g,slot),*load(g+1,1-slot))
        return 0
    lax.fori_loop(0,groups-1,body,0)
    drive(raise_(groups-1,(groups-1)&1))
    per=4
    def mm(ap):
        parts=[]
        for jj in range(per):
            a=per*ap+jj
            parts+=[jnp.concatenate([lift.at[q][pl.ds(a*blk+rr,8,stride=seg+1),:] for rr in range(seg)],0) for q in range(chunks)]
        hi,lo=split(jnp.concatenate(parts,1))
        kw=per*chunks*128
        return jnp.dot(jnp.concatenate([hi,lo],0),gv[pl.ds(pl.multiple_of(ap*kw,kw),kw),:],preferred_element_type=F32)
    accr[...]=mm(0)
    def st(ap,_):
        accr[...]+=mm(ap); return 0
    lax.fori_loop(1,na//per,st,0)
    acc=accr[...]
    tot=(acc[:nb,:ni]+acc[nb:,:ni])+(acc[:nb,ni:]+acc[nb:,ni:])
    for i0 in range(0,ni,128):
        for rr in range(seg):
            perm.at[i0//128][pl.ds(rr,8,stride=seg),:]=tot[rr*8:rr*8+8,i0:i0+128]
        turned[i0:i0+128,:]=perm[i0//128,:nb].T
    rows=outs[0].shape[0]
    for k in range(parts):
        outs[k][...]=turned[pl.ds(pl.multiple_of((lax.axis_index("alpha")^k)*rows,rows),rows),:]


def sig(c,tg,sg,pr,g,parts):
    _,na,_=c[0].shape; exc,nb=tg.shape; chunks=g.shape[0]//na//128; ni=g.shape[1]//2
    ew=(exc+127)//128*128
    vm=pl.BlockSpec(memory_space=pltpu.VMEM)
    return pl.pallas_call(functools.partial(sig_kernel,parts,len(c)),
       out_shape=[jax.ShapeDtypeStruct((ni//parts,nb),F32)]*parts,
       in_specs=[vm]*(4+len(c)),out_specs=[vm]*parts,
       scratch_shapes=[pltpu.VMEM((nb,ew),I32),pltpu.VMEM((nb,ew),F32),pltpu.VMEM((nb,ew),I32),pltpu.VMEM((2*na,256*max(PAIRED,1)),BF),pltpu.VMEM((2,BLOCK,na,ew),F32),pltpu.VMEM((2,BLOCK,na,ew),F32),
          pltpu.VMEM((chunks,(na+1)*(8*(nb//8+1)+1),128),F32),pltpu.VMEM((ni//128,nb+nb//8,128),F32),pltpu.VMEM((ni,nb),F32),pltpu.VMEM((2*nb,2*ni),F32)],
       compiler_params=pltpu.CompilerParams(vmem_limit_bytes=GRANT_B))(*c,tg,sg,pr,g)


def local(
    coeff, integrals, beta_pairs, beta_targets, beta_signs, alpha_pairs, alpha_targets, alpha_signs
):
    n_beta = lax.axis_size("beta")
    n_alpha = lax.axis_size("alpha")
    rows, _ = coeff.shape
    other = lax.ppermute(coeff, "beta", [(i, i ^ 1) for i in range(n_beta)])
    vcat, tabs = prepare(integrals, alpha_pairs, alpha_targets, alpha_signs)
    tables = [jnp.stack([coeff, other])]
    for k in range(2, n_beta, 2):
        tables.append(lax.ppermute(tables[0], "beta", [(i, i ^ k) for i in range(n_beta)]))
    g = fold(vcat, tabs, rows * n_alpha)
    parts = sig(tables, beta_targets.T, beta_signs.T, beta_pairs.T, g, n_alpha)
    total = parts[0]
    for k in range(1, n_alpha):
        total = total + lax.ppermute(parts[k], "alpha", [(i, i ^ k) for i in range(n_alpha)])
    return total


def solution(mesh):
    placed = (
        P("alpha", "beta"),
        P(),
        P("beta", None),
        P("beta", None),
        P("beta", None),
        P("alpha", None),
        P("alpha", None),
        P("alpha", None),
    )

    return jax.shard_map(local, mesh=mesh, in_specs=placed, out_specs=P("alpha", "beta"), check_vma=False)
```

time: 45.8 us -> 40.1 us (0.88)
  Pallas kernels: 29 us -> 26.3 us
  local copies, waits for them, and re-layouts: 2.03 us -> 0.01 us
  other arithmetic: 1.94 us -> 0.62 us
    ppermute x0 -> x4, starting transfers between devices: none -> 7.67 us  [the longest x3 4.7 us: local(): lax.ppermute(tables[0], 'beta', [(i, i ^ k) for i in range(n_beta)])]
    all_to_all x1 -> x0, starting transfers between devices: 7.28 us -> none  [local(): table = lax.all_to_all(table, 'beta', 0, 0)]
    pallas_call x2 -> x3, Pallas kernels: 29 us -> 26.3 us  [the longest x1 14.7 us: sig(): pl.pallas_call(functools.partial(sig_kernel, parts, len(c)), out_shape=[j...]
    broadcast_in_dim x1 -> x0, local copies, waits for them, and re-layouts: 1.38 us -> none  [local(): table = jnp.broadcast_to(coeff[None], (n_beta, rows, cols))]
    add x1, other arithmetic: 1.33 us -> 0.61 us  [local(): total + lax.ppermute(parts[k], 'alpha', [(i, i ^ k) for i in range(n_alph...]
    unnamed x2 -> x8, local copies, waits for them, and re-layouts: 0.65 us -> 0.01 us
    another operation x1, other arithmetic: 0.61 us -> 0.01 us  [local(): tables = [jnp.stack([coeff, other])]]
  transfers between devices with their start and end apart: 4 -> 7, of which waited for: 2 -> 3; matrix products, arithmetic and copies ran while one was open for 1% -> 0% of each run, Pallas kernels for 27% -> 29%
where the time goes in v4:
time: 40.1 us; the launch traced here: 39.9 us
  Pallas kernels  26.3 us (66%)
  starting transfers between devices  9.59 us (24%)
  waiting for transfers between devices  3.29 us (8%)
  other arithmetic  0.62 us (2%)
    pallas_call x1, Pallas kernels, sig(): pl.pallas_call(functools.partial(sig_kernel, parts, len(c)), out_shape=[j...  14.7 us
    pallas_call x1, Pallas kernels, fold(): pl.pallas_call(fold_kernel, out_shape=jax.ShapeDtypeStruct((tabs.shape[1]...  9.81 us
    ppermute x3, starting transfers between devices, local(): lax.ppermute(tables[0], 'beta', [(i, i ^ k) for i in range(n_beta)])  4.7 us
    ppermute x3, waiting for transfers between devices, local(): lax.ppermute(parts[k], 'alpha', [(i, i ^ k) for i in range(n_alpha)])  3.05 us
    ppermute x1, starting transfers between devices, local(): other = lax.ppermute(coeff, 'beta', [(i, i ^ 1) for i in range(n_beta)])  2.97 us
    ppermute x3, starting transfers between devices, local(): lax.ppermute(parts[k], 'alpha', [(i, i ^ k) for i in range(n_alpha)])  1.92 us
    pallas_call x1, Pallas kernels, prepare(): pl.pallas_call(prepare_kernel, out_shape=[jax.ShapeDtypeStruct((v.shape[0...  1.76 us
  transfers between devices with their start and end apart: 7, of which 3 were waited for; matrix products, arithmetic and copies ran while one was open for 0% of the time, Pallas kernels for 29%

profile of v4, /device:TPU:0, one launch (start us, length us, event | category | flops | bytes accessed | tf_op | source)
XLA Modules:
  0.0 39.9 jit_solution(16326252974532718670)
XLA Ops:
  0.0 0.0 copy-start.3
  0.0 3.0 %collective-permute-start = (f32[32,128]{1,0:T(8,128)}, f32[32,128]{1,0:T(8,128)S(1)}, u32[]{:S(2)}, u32[]{:S(2)}) collective-permute-start(f32[32,128]{1,0:T(8,128)} %param.8), channel_id=1, source_target_pairs={{0,1},{1,0},{2,3},{3,2},{4,5},{5,4},{6,7},{7,6},{8,9},{9,8},{10,11... | collective-permute-start | bytes 49160 | tf_op jit(solution)/shard_map/ppermute | solution.py:260
  3.0 1.8 %shard_map.82 = (bf16[528,1056]{1,0:T(8,128)(2,1)S(1)}, s32[3,32,230]{2,1,0:T(8,128)S(1)}) custom-call(f32[528,528]{1,0:T(8,128)} %v_hbm.1, s32[32,230]{1,0:T(8,128)} %pairs_hbm.1, s32[32,230]{1,0:T(8,128)} %tg_hbm.1, s32[32,230]{1,0:T(8,128)} %sg_hbm.1), custom_call_target="tpu_custom_call" | custom-call | flops 1000000 | bytes 3000000 | tf_op jit(solution)/shard_map/pallas_call | solution.py:49
  4.7 0.2 collective-permute-done
  5.0 0.0 copy-done.3
  5.0 4.1 %collective-permute-start.3 = (f32[2,32,128]{2,1,0:T(8,128)S(1)}, f32[2,32,128]{2,1,0:T(8,128)S(1)}, u32[]{:S(2)}, u32[]{:S(2)}) collective-permute-start(f32[2,32,128]{2,1,0:T(8,128)S(1)} %pad_maximum_fusion.args_0_), channel_id=1, source_target_pairs={{0,6},{1,7},{2,4},{3,5},{4,2},{5,3},{6,0},{7,1},{8,14},{9,15},{10,... | collective-permute-start | bytes 98312 | tf_op jit(solution)/shard_map/ppermute | solution.py:264
  9.0 0.0 collective-permute-start.2
  9.0 0.6 %collective-permute-start.1 = (f32[2,32,128]{2,1,0:T(8,128)S(1)}, f32[2,32,128]{2,1,0:T(8,128)S(1)}, u32[]{:S(2)}, u32[]{:S(2)}) collective-permute-start(f32[2,32,128]{2,1,0:T(8,128)S(1)} %pad_maximum_fusion.args_0_), channel_id=1, source_target_pairs={{0,2},{1,3},{2,0},{3,1},{4,6},{5,7},{6,4},{7,5},{8,10},{9,11},{10,... | collective-permute-start | bytes 98312 | tf_op jit(solution)/shard_map/ppermute | solution.py:264
  9.7 0.0 copy-start
  9.7 0.0 copy-start.1
  9.7 0.0 copy-start.2
  9.7 9.8 %shard_map.83.args_7_ = bf16[20480,256]{1,0:T(8,128)(2,1)S(1)} custom-call(bf16[528,1056]{1,0:T(8,128)(2,1)S(1)} %get-tuple-element.11.vcat, s32[3,32,230]{2,1,0:T(8,128)S(1)} %get-tuple-element.12.tabs), custom_call_target="tpu_custom_call" | custom-call | flops 10000000000 | bytes 12000000 | tf_op jit(solution)/shard_map/pallas_call | solution.py:123
  19.5 0.0 collective-permute-done.3.args_3_
  19.5 0.0 collective-permute-done.2.args_2_
  19.5 0.0 collective-permute-done.1.args_1_
  19.5 0.0 copy-done
  19.5 0.0 copy-done.1
  19.6 0.0 copy-done.2
  19.6 14.7 %shard_map.84 = (f32[32,128]{1,0:T(8,128)S(1)}, f32[32,128]{1,0:T(8,128)S(1)}, f32[32,128]{1,0:T(8,128)S(1)}, f32[32,128]{1,0:T(8,128)S(1)}) custom-call(f32[2,32,128]{2,1,0:T(8,128)S(1)} %pad_maximum_fusion.args_0_, f32[2,32,128]{2,1,0:T(8,128)S(1)} %collective-permute-done.1.args_1_, f32[2,32,128]{2,1,0:T(8,128)S(1)} %collective-permute-done.2.args_2_, ...), custom_call_target="tpu_custom_call" | custom-call | tf_op jit(solution)/shard_map/pallas_call | solution.py:246
  34.3 0.1 collective-permute-start.4
  34.4 1.7 %collective-permute-start.5 = (f32[32,128]{1,0:T(8,128)S(1)}, f32[32,128]{1,0:T(8,128)S(1)}, u32[]{:S(2)}, u32[]{:S(2)}) collective-permute-start(f32[32,128]{1,0:T(8,128)S(1)} %get-tuple-element.15), channel_id=1, source_target_pairs={{0,16},{8,24},{16,0},{24,8},{1,17},{9,25},{17,1},{25,9},{2,18},{10... | collective-permute-start | bytes 49160 | tf_op jit(solution)/shard_map/ppermute | solution.py:269
  36.1 0.1 collective-permute-start.6
  36.2 0.0 collective-permute-done.4
  36.3 2.0 %collective-permute-done.5 = f32[32,128]{1,0:T(8,128)S(1)} collective-permute-done((f32[32,128]{1,0:T(8,128)S(1)}, f32[32,128]{1,0:T(8,128)S(1)}, u32[]{:S(2)}, u32[]{:S(2)}) %collective-permute-start.5) | collective-permute-done | bytes 16416 | tf_op jit(solution)/shard_map/ppermute | solution.py:269
  38.2 1.1 %collective-permute-done.6 = f32[32,128]{1,0:T(8,128)S(1)} collective-permute-done((f32[32,128]{1,0:T(8,128)S(1)}, f32[32,128]{1,0:T(8,128)S(1)}, u32[]{:S(2)}, u32[]{:S(2)}) %collective-permute-start.6) | collective-permute-done | bytes 16416 | tf_op jit(solution)/shard_map/ppermute | solution.py:269
  39.3 0.6 %add_add_fusion = f32[32,128]{1,0:T(8,128)} fusion(f32[32,128]{1,0:T(8,128)S(1)} %collective-permute-done.6, f32[32,128]{1,0:T(8,128)S(1)} %collective-permute-done.5, f32[32,128]{1,0:T(8,128)S(1)} %get-tuple-element.13, f32[32,128]{1,0:T(8,128)S(1)} %collective-permute-done.4), kind=kLoop, calls=%fused_computation.1 | loop fusion | flops 12288 | bytes 81920 | tf_op jit(solution)/shard_map/add | solution.py:269
  (1 shorter events, 0.0 us)
Async XLA Ops:
  0.0 5.0 %copy-start.3 = (f32[32,128]{1,0:T(8,128)S(1)}, f32[32,128]{1,0:T(8,128)}, u32[]{:S(2)}) copy-start(f32[32,128]{1,0:T(8,128)} %param.8) | copy-start | bytes 49156
  0.0 5.0 %collective-permute-start = (f32[32,128]{1,0:T(8,128)}, f32[32,128]{1,0:T(8,128)S(1)}, u32[]{:S(2)}, u32[]{:S(2)}) collective-permute-start(f32[32,128]{1,0:T(8,128)} %param.8), channel_id=1, source_target_pairs={{0,1},{1,0},{2,3},{3,2},{4,5},{5,4},{6,7},{7,6},{8,9},{9,8},{10,11... | collective-permute-start | bytes 49160 | tf_op jit(solution)/shard_map/ppermute | solution.py:260
  5.0 14.5 %collective-permute-start.3 = (f32[2,32,128]{2,1,0:T(8,128)S(1)}, f32[2,32,128]{2,1,0:T(8,128)S(1)}, u32[]{:S(2)}, u32[]{:S(2)}) collective-permute-start(f32[2,32,128]{2,1,0:T(8,128)S(1)} %pad_maximum_fusion.args_0_), channel_id=1, source_target_pairs={{0,6},{1,7},{2,4},{3,5},{4,2},{5,3},{6,0},{7,1},{8,14},{9,15},{10,... | collective-permute-start | bytes 98312 | tf_op jit(solution)/shard_map/ppermute | solution.py:264
  9.0 10.5 %collective-permute-start.2 = (f32[2,32,128]{2,1,0:T(8,128)S(1)}, f32[2,32,128]{2,1,0:T(8,128)S(1)}, u32[]{:S(2)}, u32[]{:S(2)}) collective-permute-start(f32[2,32,128]{2,1,0:T(8,128)S(1)} %pad_maximum_fusion.args_0_), channel_id=1, source_target_pairs={{0,4},{1,5},{2,6},{3,7},{4,0},{5,1},{6,2},{7,3},{8,12},{9,13},{10,... | collective-permute-start | bytes 98312 | tf_op jit(solution)/shard_map/ppermute | solution.py:264
  9.0 10.5 %collective-permute-start.1 = (f32[2,32,128]{2,1,0:T(8,128)S(1)}, f32[2,32,128]{2,1,0:T(8,128)S(1)}, u32[]{:S(2)}, u32[]{:S(2)}) collective-permute-start(f32[2,32,128]{2,1,0:T(8,128)S(1)} %pad_maximum_fusion.args_0_), channel_id=1, source_target_pairs={{0,2},{1,3},{2,0},{3,1},{4,6},{5,7},{6,4},{7,5},{8,10},{9,11},{10,... | collective-permute-start | bytes 98312 | tf_op jit(solution)/shard_map/ppermute | solution.py:264
  9.7 9.9 %copy-start = (s32[128,230]{0,1:T(8,128)S(1)}, s32[128,230]{0,1:T(8,128)}, u32[]{:S(2)}) copy-start(s32[128,230]{0,1:T(8,128)} %param.11) | copy-start | bytes 353284
  9.7 9.9 %copy-start.1 = (s32[128,230]{0,1:T(8,128)S(1)}, s32[128,230]{0,1:T(8,128)}, u32[]{:S(2)}) copy-start(s32[128,230]{0,1:T(8,128)} %param.12) | copy-start | bytes 353284
  9.7 9.9 %copy-start.2 = (s32[128,230]{0,1:T(8,128)S(1)}, s32[128,230]{0,1:T(8,128)}, u32[]{:S(2)}) copy-start(s32[128,230]{0,1:T(8,128)} %param.10) | copy-start | bytes 353284
  34.3 1.9 %collective-permute-start.4 = (f32[32,128]{1,0:T(8,128)S(1)}, f32[32,128]{1,0:T(8,128)S(1)}, u32[]{:S(2)}, u32[]{:S(2)}) collective-permute-start(f32[32,128]{1,0:T(8,128)S(1)} %get-tuple-element.14), channel_id=1, source_target_pairs={{0,8},{8,0},{16,24},{24,16},{1,9},{9,1},{17,25},{25,17},{2,10},{10... | collective-permute-start | bytes 49160 | tf_op jit(solution)/shard_map/ppermute | solution.py:269
  34.4 3.8 %collective-permute-start.5 = (f32[32,128]{1,0:T(8,128)S(1)}, f32[32,128]{1,0:T(8,128)S(1)}, u32[]{:S(2)}, u32[]{:S(2)}) collective-permute-start(f32[32,128]{1,0:T(8,128)S(1)} %get-tuple-element.15), channel_id=1, source_target_pairs={{0,16},{8,24},{16,0},{24,8},{1,17},{9,25},{17,1},{25,9},{2,18},{10... | collective-permute-start | bytes 49160 | tf_op jit(solution)/shard_map/ppermute | solution.py:269
  36.1 3.2 %collective-permute-start.6 = (f32[32,128]{1,0:T(8,128)S(1)}, f32[32,128]{1,0:T(8,128)S(1)}, u32[]{:S(2)}, u32[]{:S(2)}) collective-permute-start(f32[32,128]{1,0:T(8,128)S(1)} %get-tuple-element.16), channel_id=1, source_target_pairs={{0,24},{8,16},{16,8},{24,0},{1,25},{9,17},{17,9},{25,1},{2,26},{10... | collective-permute-start | bytes 49160 | tf_op jit(solution)/shard_map/ppermute | solution.py:269

commit v5 on v4

--- a/solution.py
+++ b/solution.py
@@ -72,14 +72,14 @@
         a0 = pl.multiple_of(g * 8, 8)
         pairs8, tg8, sg8 = (tabs[k, pl.ds(a0, 8), :] for k in range(3))
 
-        def spread(jp):
-            for h in range(2):
+        def spread(jp, hs=(0, 1)):
+            for h in hs:
                 j = 2 * jp + h
                 op = one_hot(pairs8[j : j + 1, :], n_pairs, None)
                 tt = one_hot(tg8[j : j + 1, :], na, sg8[j : j + 1, :].astype(BF))
                 w = lax.dot_general(op, tt, NT, preferred_element_type=F32).astype(BF)
                 c = slice(h * na, (h + 1) * na)
-                s = jp % 2
+                s = jp % 3
                 wcat[s, 0:main, c] = w[:main]
                 wcat[s, main : 2 * main, c] = w[:main]
                 if rest:
@@ -87,7 +87,7 @@
                     wcat[s, 2 * main + rest : 2 * main + 2 * rest, c] = w[main:]
 
         def mix(jp):
-            g2 = jnp.dot(vcat[...], wcat[jp % 2], preferred_element_type=F32)
+            g2 = jnp.dot(vcat[...], wcat[jp % 3], preferred_element_type=F32)
             for h in range(2):
                 a = a0 + 2 * jp + h
                 hi, lo = split(g2[:, h * na : (h + 1) * na])
@@ -97,10 +97,11 @@
                 g_ref[pl.ds(pl.multiple_of(at + n_pairs, 16), width - n_pairs), :] = jnp.zeros((width - n_pairs, 2 * na), BF)
 
         spread(0)
+        spread(1)
         for jp in range(4):
-            if jp < 3:
-                spread(jp + 1)
             mix(jp)
+            if jp < 2:
+                spread(jp + 2)
         return 0
 
     lax.fori_loop(0, rows // 8, group, 0)
@@ -125,7 +126,7 @@
         out_shape=jax.ShapeDtypeStruct((tabs.shape[1] * width, 2 * total_rows), BF),
         in_specs=[vm] * 2,
         out_specs=vm,
-        scratch_shapes=[pltpu.VMEM((2, 2 * n_pairs, 2 * total_rows), BF)],
+        scratch_shapes=[pltpu.VMEM((3, 2 * n_pairs, 2 * total_rows), BF)],
         compiler_params=pltpu.CompilerParams(vmem_limit_bytes=GRANT_A),
         cost_estimate=pl.CostEstimate(flops=10 * 10**9, bytes_accessed=12 * 10**6, transcendentals=0),
     )(vcat, tabs)
@@ -215,7 +216,7 @@
         return 0
     lax.fori_loop(0,groups-1,body,0)
     drive(raise_(groups-1,(groups-1)&1))
-    per=4
+    per=8
     def mm(ap):
         parts=[]
         for jj in range(per):

time: 40.1 us -> 39.8 us (level)
  no operation moved by 1% of the time
where the time goes in v5:
time: 39.8 us; the launch traced here: 39.7 us
  Pallas kernels  26.1 us (66%)
  starting transfers between devices  9.59 us (24%)
  waiting for transfers between devices  3.28 us (8%)
  other arithmetic  0.62 us (2%)
    pallas_call x1, Pallas kernels, sig(): pl.pallas_call(functools.partial(sig_kernel, parts, len(c)), out_shape=[j...  14.5 us
    pallas_call x1, Pallas kernels, fold(): pl.pallas_call(fold_kernel, out_shape=jax.ShapeDtypeStruct((tabs.shape[1]...  9.82 us
    ppermute x3, starting transfers between devices, local(): lax.ppermute(tables[0], 'beta', [(i, i ^ k) for i in range(n_beta)])  4.7 us
    ppermute x3, waiting for transfers between devices, local(): lax.ppermute(parts[k], 'alpha', [(i, i ^ k) for i in range(n_alpha)])  3.04 us
    ppermute x1, starting transfers between devices, local(): other = lax.ppermute(coeff, 'beta', [(i, i ^ 1) for i in range(n_beta)])  2.97 us
    ppermute x3, starting transfers between devices, local(): lax.ppermute(parts[k], 'alpha', [(i, i ^ k) for i in range(n_alpha)])  1.92 us
    pallas_call x1, Pallas kernels, prepare(): pl.pallas_call(prepare_kernel, out_shape=[jax.ShapeDtypeStruct((v.shape[0...  1.76 us
  transfers between devices with their start and end apart: 7, of which 3 were waited for; matrix products, arithmetic and copies ran while one was open for 0% of the time, Pallas kernels for 29%

profile of v5, /device:TPU:0, one launch (start us, length us, event | category | flops | bytes accessed | tf_op | source)
XLA Modules:
  0.0 39.7 jit_solution(11525070365401483701)
XLA Ops:
  0.0 0.0 copy-start.3
  0.0 3.0 %collective-permute-start = (f32[32,128]{1,0:T(8,128)}, f32[32,128]{1,0:T(8,128)S(1)}, u32[]{:S(2)}, u32[]{:S(2)}) collective-permute-start(f32[32,128]{1,0:T(8,128)} %param.8), channel_id=1, source_target_pairs={{0,1},{1,0},{2,3},{3,2},{4,5},{5,4},{6,7},{7,6},{8,9},{9,8},{10,11... | collective-permute-start | bytes 49160 | tf_op jit(solution)/shard_map/ppermute | solution.py:261
  3.0 1.8 %shard_map.82 = (bf16[528,1056]{1,0:T(8,128)(2,1)S(1)}, s32[3,32,230]{2,1,0:T(8,128)S(1)}) custom-call(f32[528,528]{1,0:T(8,128)} %v_hbm.1, s32[32,230]{1,0:T(8,128)} %pairs_hbm.1, s32[32,230]{1,0:T(8,128)} %tg_hbm.1, s32[32,230]{1,0:T(8,128)} %sg_hbm.1), custom_call_target="tpu_custom_call" | custom-call | flops 1000000 | bytes 3000000 | tf_op jit(solution)/shard_map/pallas_call | solution.py:49
  4.7 0.2 collective-permute-done
  5.0 0.0 copy-done.3
  5.0 4.1 %collective-permute-start.3 = (f32[2,32,128]{2,1,0:T(8,128)S(1)}, f32[2,32,128]{2,1,0:T(8,128)S(1)}, u32[]{:S(2)}, u32[]{:S(2)}) collective-permute-start(f32[2,32,128]{2,1,0:T(8,128)S(1)} %pad_maximum_fusion.args_0_), channel_id=1, source_target_pairs={{0,6},{1,7},{2,4},{3,5},{4,2},{5,3},{6,0},{7,1},{8,14},{9,15},{10,... | collective-permute-start | bytes 98312 | tf_op jit(solution)/shard_map/ppermute | solution.py:265
  9.0 0.0 collective-permute-start.2
  9.0 0.6 %collective-permute-start.1 = (f32[2,32,128]{2,1,0:T(8,128)S(1)}, f32[2,32,128]{2,1,0:T(8,128)S(1)}, u32[]{:S(2)}, u32[]{:S(2)}) collective-permute-start(f32[2,32,128]{2,1,0:T(8,128)S(1)} %pad_maximum_fusion.args_0_), channel_id=1, source_target_pairs={{0,2},{1,3},{2,0},{3,1},{4,6},{5,7},{6,4},{7,5},{8,10},{9,11},{10,... | collective-permute-start | bytes 98312 | tf_op jit(solution)/shard_map/ppermute | solution.py:265
  9.7 0.0 copy-start
  9.7 0.0 copy-start.1
  9.7 0.0 copy-start.2
  9.7 9.8 %shard_map.83.args_7_ = bf16[20480,256]{1,0:T(8,128)(2,1)S(1)} custom-call(bf16[528,1056]{1,0:T(8,128)(2,1)S(1)} %get-tuple-element.11.vcat, s32[3,32,230]{2,1,0:T(8,128)S(1)} %get-tuple-element.12.tabs), custom_call_target="tpu_custom_call" | custom-call | flops 10000000000 | bytes 12000000 | tf_op jit(solution)/shard_map/pallas_call | solution.py:124
  19.5 0.0 collective-permute-done.3.args_3_
  19.5 0.0 collective-permute-done.2.args_2_
  19.5 0.0 collective-permute-done.1.args_1_
  19.5 0.0 copy-done
  19.6 0.0 copy-done.1
  19.6 0.0 copy-done.2
  19.6 14.5 %shard_map.84 = (f32[32,128]{1,0:T(8,128)S(1)}, f32[32,128]{1,0:T(8,128)S(1)}, f32[32,128]{1,0:T(8,128)S(1)}, f32[32,128]{1,0:T(8,128)S(1)}) custom-call(f32[2,32,128]{2,1,0:T(8,128)S(1)} %pad_maximum_fusion.args_0_, f32[2,32,128]{2,1,0:T(8,128)S(1)} %collective-permute-done.1.args_1_, f32[2,32,128]{2,1,0:T(8,128)S(1)} %collective-permute-done.2.args_2_, ...), custom_call_target="tpu_custom_call" | custom-call | tf_op jit(solution)/shard_map/pallas_call | solution.py:247
  34.1 0.1 collective-permute-start.4
  34.2 1.7 %collective-permute-start.5 = (f32[32,128]{1,0:T(8,128)S(1)}, f32[32,128]{1,0:T(8,128)S(1)}, u32[]{:S(2)}, u32[]{:S(2)}) collective-permute-start(f32[32,128]{1,0:T(8,128)S(1)} %get-tuple-element.15), channel_id=1, source_target_pairs={{0,16},{8,24},{16,0},{24,8},{1,17},{9,25},{17,1},{25,9},{2,18},{10... | collective-permute-start | bytes 49160 | tf_op jit(solution)/shard_map/ppermute | solution.py:270
  35.9 0.1 collective-permute-start.6
  36.0 0.0 collective-permute-done.4
  36.0 2.0 %collective-permute-done.5 = f32[32,128]{1,0:T(8,128)S(1)} collective-permute-done((f32[32,128]{1,0:T(8,128)S(1)}, f32[32,128]{1,0:T(8,128)S(1)}, u32[]{:S(2)}, u32[]{:S(2)}) %collective-permute-start.5) | collective-permute-done | bytes 16416 | tf_op jit(solution)/shard_map/ppermute | solution.py:270
  38.0 1.1 %collective-permute-done.6 = f32[32,128]{1,0:T(8,128)S(1)} collective-permute-done((f32[32,128]{1,0:T(8,128)S(1)}, f32[32,128]{1,0:T(8,128)S(1)}, u32[]{:S(2)}, u32[]{:S(2)}) %collective-permute-start.6) | collective-permute-done | bytes 16416 | tf_op jit(solution)/shard_map/ppermute | solution.py:270
  39.1 0.6 %add_add_fusion = f32[32,128]{1,0:T(8,128)} fusion(f32[32,128]{1,0:T(8,128)S(1)} %collective-permute-done.6, f32[32,128]{1,0:T(8,128)S(1)} %collective-permute-done.5, f32[32,128]{1,0:T(8,128)S(1)} %get-tuple-element.13, f32[32,128]{1,0:T(8,128)S(1)} %collective-permute-done.4), kind=kLoop, calls=%fused_computation.1 | loop fusion | flops 12288 | bytes 81920 | tf_op jit(solution)/shard_map/add | solution.py:270
  (1 shorter events, 0.0 us)
Async XLA Ops:
  0.0 5.0 %copy-start.3 = (f32[32,128]{1,0:T(8,128)S(1)}, f32[32,128]{1,0:T(8,128)}, u32[]{:S(2)}) copy-start(f32[32,128]{1,0:T(8,128)} %param.8) | copy-start | bytes 49156
  0.0 5.0 %collective-permute-start = (f32[32,128]{1,0:T(8,128)}, f32[32,128]{1,0:T(8,128)S(1)}, u32[]{:S(2)}, u32[]{:S(2)}) collective-permute-start(f32[32,128]{1,0:T(8,128)} %param.8), channel_id=1, source_target_pairs={{0,1},{1,0},{2,3},{3,2},{4,5},{5,4},{6,7},{7,6},{8,9},{9,8},{10,11... | collective-permute-start | bytes 49160 | tf_op jit(solution)/shard_map/ppermute | solution.py:261
  5.0 14.5 %collective-permute-start.3 = (f32[2,32,128]{2,1,0:T(8,128)S(1)}, f32[2,32,128]{2,1,0:T(8,128)S(1)}, u32[]{:S(2)}, u32[]{:S(2)}) collective-permute-start(f32[2,32,128]{2,1,0:T(8,128)S(1)} %pad_maximum_fusion.args_0_), channel_id=1, source_target_pairs={{0,6},{1,7},{2,4},{3,5},{4,2},{5,3},{6,0},{7,1},{8,14},{9,15},{10,... | collective-permute-start | bytes 98312 | tf_op jit(solution)/shard_map/ppermute | solution.py:265
  9.0 10.5 %collective-permute-start.2 = (f32[2,32,128]{2,1,0:T(8,128)S(1)}, f32[2,32,128]{2,1,0:T(8,128)S(1)}, u32[]{:S(2)}, u32[]{:S(2)}) collective-permute-start(f32[2,32,128]{2,1,0:T(8,128)S(1)} %pad_maximum_fusion.args_0_), channel_id=1, source_target_pairs={{0,4},{1,5},{2,6},{3,7},{4,0},{5,1},{6,2},{7,3},{8,12},{9,13},{10,... | collective-permute-start | bytes 98312 | tf_op jit(solution)/shard_map/ppermute | solution.py:265
  9.0 10.5 %collective-permute-start.1 = (f32[2,32,128]{2,1,0:T(8,128)S(1)}, f32[2,32,128]{2,1,0:T(8,128)S(1)}, u32[]{:S(2)}, u32[]{:S(2)}) collective-permute-start(f32[2,32,128]{2,1,0:T(8,128)S(1)} %pad_maximum_fusion.args_0_), channel_id=1, source_target_pairs={{0,2},{1,3},{2,0},{3,1},{4,6},{5,7},{6,4},{7,5},{8,10},{9,11},{10,... | collective-permute-start | bytes 98312 | tf_op jit(solution)/shard_map/ppermute | solution.py:265
  9.7 9.9 %copy-start = (s32[128,230]{0,1:T(8,128)S(1)}, s32[128,230]{0,1:T(8,128)}, u32[]{:S(2)}) copy-start(s32[128,230]{0,1:T(8,128)} %param.11) | copy-start | bytes 353284
  9.7 9.9 %copy-start.1 = (s32[128,230]{0,1:T(8,128)S(1)}, s32[128,230]{0,1:T(8,128)}, u32[]{:S(2)}) copy-start(s32[128,230]{0,1:T(8,128)} %param.12) | copy-start | bytes 353284
  9.7 9.9 %copy-start.2 = (s32[128,230]{0,1:T(8,128)S(1)}, s32[128,230]{0,1:T(8,128)}, u32[]{:S(2)}) copy-start(s32[128,230]{0,1:T(8,128)} %param.10) | copy-start | bytes 353284
  34.1 1.9 %collective-permute-start.4 = (f32[32,128]{1,0:T(8,128)S(1)}, f32[32,128]{1,0:T(8,128)S(1)}, u32[]{:S(2)}, u32[]{:S(2)}) collective-permute-start(f32[32,128]{1,0:T(8,128)S(1)} %get-tuple-element.14), channel_id=1, source_target_pairs={{0,8},{8,0},{16,24},{24,16},{1,9},{9,1},{17,25},{25,17},{2,10},{10... | collective-permute-start | bytes 49160 | tf_op jit(solution)/shard_map/ppermute | solution.py:270
  34.2 3.8 %collective-permute-start.5 = (f32[32,128]{1,0:T(8,128)S(1)}, f32[32,128]{1,0:T(8,128)S(1)}, u32[]{:S(2)}, u32[]{:S(2)}) collective-permute-start(f32[32,128]{1,0:T(8,128)S(1)} %get-tuple-element.15), channel_id=1, source_target_pairs={{0,16},{8,24},{16,0},{24,8},{1,17},{9,25},{17,1},{25,9},{2,18},{10... | collective-permute-start | bytes 49160 | tf_op jit(solution)/shard_map/ppermute | solution.py:270
  35.9 3.2 %collective-permute-start.6 = (f32[32,128]{1,0:T(8,128)S(1)}, f32[32,128]{1,0:T(8,128)S(1)}, u32[]{:S(2)}, u32[]{:S(2)}) collective-permute-start(f32[32,128]{1,0:T(8,128)S(1)} %get-tuple-element.16), channel_id=1, source_target_pairs={{0,24},{8,16},{16,8},{24,0},{1,25},{9,17},{17,9},{25,1},{2,26},{10... | collective-permute-start | bytes 49160 | tf_op jit(solution)/shard_map/ppermute | solution.py:270
